TPU v7x, 128 devices: a whole 4x4x4 slice. The times are simulated.
128 devices in a mesh: dp: 2 (over core), expert: 64 (over z, y, x).
Axes of the slice: x: 4, y: 4, z: 4, core: 2. Of those that a mesh axis runs over, the one named last changes fastest.
Arguments:
- tokens: bfloat16 [8192, 1792], P(('dp', 'expert')), may hold values from -6 to 6
- grad_out: bfloat16 [8192, 1792], P(('dp', 'expert')), may hold values from -6 to 6
- combine: float32 [8192, 8], P(('dp', 'expert')), may hold values from 0.02 to 0.3
- expert_ids: int32 [8192, 8], P(('dp', 'expert')), may hold values from 0 to 63, all different within a row; in each aligned block of 64 rows (0 to 63, 64 to 127, ...) at most 12 rows name the same one
- w_gate: bfloat16 [64, 1792, 1280], P('expert', 'dp'), may hold values from -0.125 to 0.125
- w_up: bfloat16 [64, 1792, 1280], P('expert', 'dp'), may hold values from -0.125 to 0.125
- w_down: bfloat16 [64, 1792, 1280], P('expert', 'dp'), may hold values from -0.15625 to 0.15625
Outputs:
- token_grad: bfloat16 [8192, 1792], P(('dp', 'expert'))
- grad_w_gate: bfloat16 [64, 1792, 1280], P('expert', 'dp')
- grad_w_up: bfloat16 [64, 1792, 1280], P('expert', 'dp')
- grad_w_down: bfloat16 [64, 1792, 1280], P('expert', 'dp')
Inputs may be any that keep to these rules, and one draw needn't show every extreme that they name: `expert_ids`: each row names 8 different experts; within the rows of one device no expert is named more than 12 times.
All inputs are finite; a program needn't handle non-finite values.
Results may differ from a plain program's by a relative error of at most 0.0066.
Values may be sent and summed in bfloat16 or wider, within the bound.
A program may use at most 128 MiB of HBM per device.

v0:
```python
import jax
import jax.numpy as jnp
from jax import lax
from jax.sharding import PartitionSpec as P


def sent_together(arrays, axis, split_dim, concat_dim, along):
    widths = [a.shape[along] for a in arrays]
    both = jnp.concatenate(arrays, axis=along)
    whole = lax.all_to_all(both, axis, split_axis=split_dim, concat_axis=concat_dim, tiled=True)
    return tuple(jnp.split(whole, [sum(widths[:k]) for k in range(1, len(widths))], axis=along))


def in_one_piece(arrays, axis, dim, along):
    both = jnp.concatenate(arrays, axis=along)
    whole, at, outs = (lax.all_gather(both, axis, axis=dim, tiled=True), 0, [])
    for a in arrays:
        outs.append(lax.slice_in_dim(whole, at, at + a.shape[along], axis=along))
        at += a.shape[along]
    return tuple(outs)


def expert_backward(expert_in, expert_grad_in, gate_mat, up_mat, down_mat):
    gate_pre = jnp.dot(expert_in, gate_mat, preferred_element_type=jnp.float32)
    up_pre = jnp.dot(expert_in, up_mat, preferred_element_type=jnp.float32)
    sigmoid_gate = jax.nn.sigmoid(gate_pre)
    gate_act = gate_pre * sigmoid_gate
    hidden = (gate_act * up_pre).astype(jnp.bfloat16)
    grad_hidden = jnp.dot(expert_grad_in, down_mat, preferred_element_type=jnp.float32)
    grad_gate = (
        grad_hidden * up_pre * sigmoid_gate * (1.0 + gate_pre * (1.0 - sigmoid_gate))
    ).astype(jnp.bfloat16)
    grad_up = (grad_hidden * gate_act).astype(jnp.bfloat16)
    contract = (((1,), (1,)), ((), ()))
    grad_x = lax.dot_general(grad_gate, gate_mat, contract, preferred_element_type=jnp.float32)
    grad_x = grad_x + lax.dot_general(grad_up, up_mat, contract, preferred_element_type=jnp.float32)
    return (hidden, grad_gate, grad_up, grad_x.astype(jnp.bfloat16))


def replica_terms(expert_in, expert_grad_in, hidden, grad_gate, grad_up):
    contract = (((0,), (0,)), ((), ()))
    terms = jnp.concatenate(
        [
            lax.dot_general(expert_in, grad_gate, contract, preferred_element_type=jnp.float32),
            lax.dot_general(expert_in, grad_up, contract, preferred_element_type=jnp.float32),
            lax.dot_general(expert_grad_in, hidden, contract, preferred_element_type=jnp.float32),
        ],
        axis=1,
    )
    rounded = lax.optimization_barrier(terms.astype(jnp.bfloat16))
    return rounded.astype(jnp.float32)


def shards(tokens, grad_out, combine, expert_ids, w_gate, w_up, w_down):
    experts = lax.axis_size("expert")
    tok_count, top_count = expert_ids.shape
    capacity = min(tok_count, max(2, 3 * tok_count * top_count // (2 * experts)))
    slot_rows = experts * capacity
    assigns = tok_count * top_count
    flat_ids = expert_ids.reshape(assigns).astype(jnp.float32)
    onehot = (flat_ids[:, None] == jnp.arange(experts, dtype=jnp.float32)[None, :]).astype(
        jnp.float32
    )
    strict_below = (jnp.arange(assigns)[:, None] > jnp.arange(assigns)[None, :]).astype(jnp.float32)
    earlier = jnp.dot(strict_below, onehot, precision=lax.Precision.HIGHEST)
    slot_rank = jnp.sum(earlier * onehot, axis=1)
    position = flat_ids * capacity + slot_rank
    placed = (jnp.arange(slot_rows, dtype=jnp.float32)[:, None] == position[None, :]).astype(
        jnp.float32
    )
    dispatch = placed.reshape(slot_rows, tok_count, top_count).sum(axis=2).astype(jnp.bfloat16)
    weighted = (
        (placed * combine.reshape(assigns)[None, :])
        .reshape(slot_rows, tok_count, top_count)
        .sum(axis=2)
    )
    sent_rows = jnp.dot(dispatch, tokens, preferred_element_type=jnp.float32).astype(jnp.bfloat16)
    sent_grads = jnp.dot(
        weighted, grad_out.astype(jnp.float32), precision=lax.Precision.HIGHEST
    ).astype(jnp.bfloat16)
    expert_in, expert_grad_in = sent_together((sent_rows, sent_grads), "expert", 0, 0, 1)
    gate_full, up_full, down_full = in_one_piece((w_gate, w_up, w_down), "dp", 1, 0)
    hidden, grad_gate, grad_up, grad_x = expert_backward(
        expert_in, expert_grad_in, gate_full[0], up_full[0], down_full[0]
    )
    returned = lax.all_to_all(grad_x, "expert", split_axis=0, concat_axis=0, tiled=True)
    token_grad = lax.dot_general(
        dispatch, returned, (((0,), (0,)), ((), ())), preferred_element_type=jnp.float32
    ).astype(jnp.bfloat16)
    own_rows = w_gate.shape[1]
    width = grad_gate.shape[1]
    x_quarter, grad_quarter = (
        lax.all_to_all(expert_in, "dp", split_axis=1, concat_axis=0, tiled=True),
        lax.all_to_all(expert_grad_in, "dp", split_axis=1, concat_axis=0, tiled=True),
    )
    routed = expert_in.shape[0]
    initial = jnp.zeros((own_rows, 3 * width), jnp.float32)
    summed = initial
    first_row = jnp.int32(0)
    gate_piece = lax.all_gather(grad_gate, "dp", axis=0, tiled=True)
    up_piece = lax.all_gather(grad_up, "dp", axis=0, tiled=True)
    hidden_piece = lax.all_gather(hidden, "dp", axis=0, tiled=True)
    for member in range(gate_piece.shape[0] // routed):
        offset = first_row + member * routed
        x_rows = lax.dynamic_slice_in_dim(x_quarter, offset, routed, 0)
        grad_rows_here = lax.dynamic_slice_in_dim(grad_quarter, offset, routed, 0)
        lower_row = member * routed
        upper_row = lower_row + routed
        summed = summed + replica_terms(
            x_rows,
            grad_rows_here,
            hidden_piece[lower_row:upper_row],
            gate_piece[lower_row:upper_row],
            up_piece[lower_row:upper_row],
        )
    grad_w_gate = summed[:, :width].astype(jnp.bfloat16)[None]
    grad_w_up = summed[:, width : 2 * width].astype(jnp.bfloat16)[None]
    grad_w_down = summed[:, 2 * width :].astype(jnp.bfloat16)[None]
    return (token_grad, grad_w_gate, grad_w_up, grad_w_down)


def solution(mesh):
    in_specs = (
        P(("dp", "expert"), None),
        P(("dp", "expert"), None),
        P(("dp", "expert"), None),
        P(("dp", "expert"), None),
        P("expert", "dp", None),
        P("expert", "dp", None),
        P("expert", "dp", None),
    )
    out_specs = (
        P(("dp", "expert"), None),
        P("expert", "dp", None),
        P("expert", "dp", None),
        P("expert", "dp", None),
    )
    return jax.shard_map(shards, mesh=mesh, in_specs=in_specs, out_specs=out_specs, check_vma=False)
```

profile of v0, /device:TPU:1, one launch (start us, length us, event | category | flops | bytes accessed | tf_op | source)
XLA Modules:
  0.0 301.1 jit_solution(12773531230361914865)
XLA Ops:
  7.2 6.4 %pad_maximum_fusion = bf16[3,896,1280]{2,1,0:T(8,128)(2,1)} fusion(bf16[1,896,1280]{2,1,0:T(8,128)(2,1)} %param.13, bf16[1,896,1280]{2,1,0:T(8,128)(2,1)} %param.12, bf16[1,896,1280]{2,1,0:T(8,128)(2,1)} %param.11), kind=kLoop, calls=%fused_computation.1 | loop fusion | flops 6881280 | bytes 13762560 | tf_op jit(solution)/shard_map/concatenate | solution.py:15
  16.8 2.4 convolution_convert_fusion.6
  19.2 2.8 pad_maximum_fusion.3
  22.1 9.6 %all_to_all.40 = bf16[64,12,3584]{2,1,0:T(8,128)(2,1)} reshape(bf16[768,3584]{1,0:T(8,128)(2,1)} %pad_maximum_fusion.3) | data formatting | bytes 11010048 | tf_op jit(solution)/shard_map/all_to_all | solution.py:10
  31.7 97.5 %all_to_all.56 = bf16[64,12,3584]{2,1,0:T(8,128)(2,1)} all-to-all(bf16[64,12,3584]{2,1,0:T(8,128)(2,1)} %all_to_all.40), channel_id=1, replica_groups=mesh['dp'=2,'expert'=64] {'expert'}, dimensions={0} | all-to-all | bytes 11010048 | tf_op jit(solution)/shard_map/all_to_all | solution.py:10
  129.2 9.4 %all_to_all.42 = bf16[768,3584]{1,0:T(8,128)(2,1)} reshape(bf16[64,12,3584]{2,1,0:T(8,128)(2,1)} %all_to_all.56) | data formatting | bytes 11010048 | tf_op jit(solution)/shard_map/all_to_all | solution.py:10
  138.5 7.0 %fusion.4 = f32[768,1280]{1,0:T(8,128)S(1)} fusion(bf16[3,1792,1280]{2,1,0:T(8,128)(2,1)} %all-gather.5.cloned.1.call-done, bf16[768,3584]{1,0:T(8,128)(2,1)} %all_to_all.42), kind=kOutput, calls=%fused_computation.13 | convolution fusion | flops 3523215360 | bytes 11272192 | tf_op jit(solution)/shard_map/dot_general | solution.py:24
  145.5 1.7 copy-done.10
  147.2 5.6 %fusion = f32[768,1280]{1,0:T(8,128)} fusion(bf16[3,1792,1280]{2,1,0:T(8,128)(2,1)S(1)} %copy-done.10, bf16[768,3584]{1,0:T(8,128)(2,1)S(1)} %copy-done.2), kind=kOutput, calls=%fused_computation.9 | convolution fusion | flops 3523215360 | bytes 11272192 | tf_op jit(solution)/shard_map/dot_general | solution.py:29
  152.9 8.8 %multiply_convert_fusion = (bf16[768,1280]{1,0:T(8,128)(2,1)}, bf16[768,1280]{1,0:T(8,128)(2,1)}, bf16[768,1280]{1,0:T(8,128)(2,1)}) fusion(f32[768,1280]{1,0:T(8,128)S(1)} %fusion.4, f32[768,1280]{1,0:T(8,128)} %fusion, bf16[3,1792,1280]{2,1,0:T(8,128)(2,1)S(1)} %copy-done.10, bf16[768,3584]{1,0:T(8,128)(2,1)S(1)} %copy-done.2), kind=kOutput, calls=%fused_computation.14 | convolution fusion | flops 3537960960 | bytes 21102592 | tf_op jit(solution)/shard_map/dot_general | solution.py:25
  163.2 6.2 %fusion.1 = f32[768,1792]{1,0:T(8,128)S(1)} fusion(bf16[768,1280]{1,0:T(8,128)(2,1)S(1)} %copy-done.6, bf16[3,1792,1280]{2,1,0:T(8,128)(2,1)} %all-gather.5.cloned.1.call-done), kind=kOutput, calls=%fused_computation.10 | convolution fusion | flops 3523215360 | bytes 12058624 | tf_op jit(solution)/shard_map/dot_general | solution.py:36
  169.4 7.0 %add_convert_fusion.1 = bf16[768,1792]{1,0:T(8,128)(2,1)S(1)} fusion(f32[768,1792]{1,0:T(8,128)S(1)} %fusion.1, bf16[768,1280]{1,0:T(8,128)(2,1)S(1)} %copy-done.5, bf16[3,1792,1280]{2,1,0:T(8,128)(2,1)} %all-gather.5.cloned.1.call-done), kind=kOutput, calls=%fused_computation.5 | convolution fusion | flops 3525967872 | bytes 14811136 | tf_op jit(solution)/shard_map/dot_general | solution.py:35
  176.4 2.5 all_to_all.43
  178.9 6.7 %all-to-all-start.1 = ((bf16[64,12,1792]{2,1,0:T(8,128)(2,1)}), bf16[64,12,1792]{2,1,0:T(8,128)(2,1)}, u32[]{:S(2)}, u32[]{:S(2)}) async-start(bf16[64,12,1792]{2,1,0:T(8,128)(2,1)} %all_to_all.43), calls=%async_computation.1 | async-start | bytes 7340032 | tf_op jit(solution)/shard_map/all_to_all | solution.py:86
  186.2 3.1 %fusion.19 = (bf16[768,1792]{1,0:T(8,128)(2,1)S(1)}, bf16[768,1792]{1,0:T(8,128)(2,1)S(1)}) fusion(bf16[768,3584]{1,0:T(8,128)(2,1)} %all_to_all.42), kind=kLoop, calls=%fused_computation.57 | loop fusion | bytes 11010048 | tf_op jit(solution)/shard_map/split | solution.py:11
  189.3 1.8 copy.25
  191.1 1.7 copy.26
  192.8 37.7 %all-to-all-done.1 = bf16[64,12,1792]{2,1,0:T(8,128)(2,1)} async-done(((bf16[64,12,1792]{2,1,0:T(8,128)(2,1)}), bf16[64,12,1792]{2,1,0:T(8,128)(2,1)}, u32[]{:S(2)}, u32[]{:S(2)}) %all-to-all-start.1) | async-done | bytes 2752544 | tf_op jit(solution)/shard_map/all_to_all | solution.py:86
  230.6 8.6 %all-to-all-start.2 = ((bf16[768,2,896]{2,0,1:T(8,128)(2,1)}), bf16[768,2,896]{2,0,1:T(8,128)(2,1)}, u32[]{:S(2)}, u32[]{:S(2)}) async-start(bf16[768,2,896]{2,0,1:T(8,128)(2,1)} %bitcast.52), calls=%async_computation.2 | async-start | bytes 5505024 | tf_op jit(solution)/shard_map/all_to_all | solution.py:93
  239.2 3.8 %all_to_all.45 = bf16[768,1792]{1,0:T(8,128)(2,1)S(1)} reshape(bf16[64,12,1792]{2,1,0:T(8,128)(2,1)} %all-to-all-done.1) | data formatting | bytes 5505024 | tf_op jit(solution)/shard_map/all_to_all | solution.py:86
  243.0 1.3 convolution_convert_fusion.8
  244.3 3.9 %all-to-all-start.3 = ((bf16[768,2,896]{2,0,1:T(8,128)(2,1)}), bf16[768,2,896]{2,0,1:T(8,128)(2,1)S(1)}, u32[]{:S(2)}, u32[]{:S(2)}) async-start(bf16[768,2,896]{2,0,1:T(8,128)(2,1)} %bitcast.51), calls=%async_computation.3 | async-start | bytes 5505024 | tf_op jit(solution)/shard_map/all_to_all | solution.py:94
  248.2 5.3 %convolution_convert_fusion.1 = bf16[896,1280]{1,0:T(8,128)(2,1)} fusion(bf16[1536,1280]{1,0:T(8,128)(2,1)} %all-gather.9.cloned.1.call-done, bf16[2,768,896]{2,1,0:T(8,128)(2,1)} %bitcast.3), kind=kOutput, calls=%fused_computation.20 | convolution fusion | flops 1762754560 | bytes 5636096 | tf_op jit(solution)/shard_map/dot_general | solution.py:45
  253.6 5.3 %convolution_convert_fusion.2 = bf16[896,1280]{1,0:T(8,128)(2,1)} fusion(bf16[1536,1280]{1,0:T(8,128)(2,1)} %all-gather.7.cloned.1.call-done, bf16[2,768,896]{2,1,0:T(8,128)(2,1)} %bitcast.3), kind=kOutput, calls=%fused_computation.21 | convolution fusion | flops 1762754560 | bytes 5636096 | tf_op jit(solution)/shard_map/dot_general | solution.py:44
  258.9 3.7 %convolution_convert_fusion = bf16[896,1280]{1,0:T(8,128)(2,1)S(1)} fusion(bf16[1536,1280]{1,0:T(8,128)(2,1)} %all-gather.11.cloned.1.call-done, bf16[2,768,896]{2,1,0:T(8,128)(2,1)S(1)} %bitcast.55), kind=kOutput, calls=%fused_computation.19 | convolution fusion | flops 1762754560 | bytes 5636096 | tf_op jit(solution)/shard_map/dot_general | solution.py:46
  262.6 3.6 %pad_maximum_fusion.2 = bf16[896,3840]{1,0:T(8,128)(2,1)} fusion(bf16[896,1280]{1,0:T(8,128)(2,1)S(1)} %convolution_convert_fusion, bf16[896,1280]{1,0:T(8,128)(2,1)S(1)} %copy-done.3, bf16[896,1280]{1,0:T(8,128)(2,1)S(1)} %copy-done.4), kind=kLoop, calls=%fused_computation.3 | loop fusion | flops 20643840 | bytes 13762560 | tf_op jit(solution)/shard_map/concatenate | solution.py:42
  266.6 2.0 convolution_convert_fusion.3
  268.7 3.5 %convolution_convert_fusion.4 = bf16[896,1280]{1,0:T(8,128)(2,1)S(1)} fusion(bf16[1536,1280]{1,0:T(8,128)(2,1)S(1)} %copy-done.11, bf16[2,768,896]{2,1,0:T(8,128)(2,1)} %bitcast.3), kind=kOutput, calls=%fused_computation.23 | convolution fusion | flops 1762754560 | bytes 5636096 | tf_op jit(solution)/shard_map/dot_general | solution.py:45
  272.2 3.3 %convolution_convert_fusion.5 = bf16[896,1280]{1,0:T(8,128)(2,1)S(1)} fusion(bf16[1536,1280]{1,0:T(8,128)(2,1)S(1)} %copy-done.12, bf16[2,768,896]{2,1,0:T(8,128)(2,1)} %bitcast.3), kind=kOutput, calls=%fused_computation.24 | convolution fusion | flops 1762754560 | bytes 5636096 | tf_op jit(solution)/shard_map/dot_general | solution.py:44
  275.6 3.4 %pad_maximum_fusion.1 = bf16[896,3840]{1,0:T(8,128)(2,1)} fusion(bf16[896,1280]{1,0:T(8,128)(2,1)S(1)} %convolution_convert_fusion.3, bf16[896,1280]{1,0:T(8,128)(2,1)S(1)} %convolution_convert_fusion.4, bf16[896,1280]{1,0:T(8,128)(2,1)S(1)} %convolution_convert_fusion.5), kind=kLoop, calls=%fused_computation.2 | loop fusion | flops 20643840 | bytes 13762560 | tf_op jit(solution)/shard_map/concatenate | solution.py:42
  279.0 9.4 %add_convert_fusion = bf16[896,3840]{1,0:T(8,128)(2,1)} fusion(bf16[896,3840]{1,0:T(8,128)(2,1)} %pad_maximum_fusion.2, bf16[896,3840]{1,0:T(8,128)(2,1)} %pad_maximum_fusion.1), kind=kLoop, calls=%fused_computation | loop fusion | flops 13762560 | bytes 20643840 | tf_op jit(solution)/shard_map/convert.2
  288.4 6.1 %slice_bitcast_fusion.10 = (bf16[1,896,1280]{2,1,0:T(8,128)(2,1)}, bf16[1,896,1280]{2,1,0:T(8,128)(2,1)}, bf16[1,896,1280]{2,1,0:T(8,128)(2,1)}) fusion(bf16[896,3840]{1,0:T(8,128)(2,1)} %add_convert_fusion), kind=kLoop, calls=%fused_computation.30 | loop fusion | bytes 13762560 | tf_op jit(solution)/shard_map/broadcast_in_dim | solution.py:118
  (50 shorter events, 5.9 us)
Async XLA Ops:
  7.2 8.8 %copy-start = (bf16[64,1792]{1,0:T(8,128)(2,1)S(1)}, bf16[64,1792]{1,0:T(8,128)(2,1)}, u32[]{:S(2)}) copy-start(bf16[64,1792]{1,0:T(8,128)(2,1)} %param.7) | copy-start | bytes 688132
  7.2 131.3 %all-gather.5.cloned.1.call-start = ((), (), s32[]{:S(2)}) async-start(), calls=%async_computation.4 | async-start | bytes 20643840 | tf_op jit(solution)/shard_map/all_gather | solution.py:16
  13.6 0.7 copy-start.8
  13.6 1.3 copy-start.9
  13.6 3.2 %copy-start.7 = (bf16[64,1792]{1,0:T(8,128)(2,1)S(1)}, bf16[64,1792]{1,0:T(8,128)(2,1)}, u32[]{:S(2)}) copy-start(bf16[64,1792]{1,0:T(8,128)(2,1)} %param.8) | copy-start | bytes 688132
  13.6 234.6 %all-gather.9.cloned.1.call-start = ((), (), s32[]{:S(2)}) async-start(), calls=%async_computation.6 | async-start | bytes 5898240 | tf_op jit(solution)/shard_map/all_gather | solution.py:101
  138.5 7.0 %copy-start.2 = (bf16[768,3584]{1,0:T(8,128)(2,1)S(1)}, bf16[768,3584]{1,0:T(8,128)(2,1)}, u32[]{:S(2)}) copy-start(bf16[768,3584]{1,0:T(8,128)(2,1)} %all_to_all.42) | copy-start | bytes 16515076
  138.5 8.7 %copy-start.10 = (bf16[3,1792,1280]{2,1,0:T(8,128)(2,1)S(1)}, bf16[3,1792,1280]{2,1,0:T(8,128)(2,1)}, u32[]{:S(2)}) copy-start(bf16[3,1792,1280]{2,1,0:T(8,128)(2,1)} %all-gather.5.cloned.1.call-done) | copy-start | bytes 41287684
  161.7 1.5 copy-start.6
  161.7 91.8 %all-gather.7.cloned.1.call-start = ((), (), s32[]{:S(2)}) async-start(), calls=%async_computation.5 | async-start | bytes 5898240 | tf_op jit(solution)/shard_map/all_gather | solution.py:100
  163.2 6.2 %copy-start.5 = (bf16[768,1280]{1,0:T(8,128)(2,1)S(1)}, bf16[768,1280]{1,0:T(8,128)(2,1)}, u32[]{:S(2)}) copy-start(bf16[768,1280]{1,0:T(8,128)(2,1)} %get-tuple-element.7) | copy-start | bytes 5898244
  178.9 51.7 %all-to-all-start.1 = ((bf16[64,12,1792]{2,1,0:T(8,128)(2,1)}), bf16[64,12,1792]{2,1,0:T(8,128)(2,1)}, u32[]{:S(2)}, u32[]{:S(2)}) async-start(bf16[64,12,1792]{2,1,0:T(8,128)(2,1)} %all_to_all.43), calls=%async_computation.1 | async-start | bytes 7340032 | tf_op jit(solution)/shard_map/all_to_all | solution.py:86
  185.6 73.3 %all-gather.11.cloned.1.call-start = ((), (), s32[]{:S(2)}) async-start(), calls=%async_computation.7 | async-start | bytes 5898240 | tf_op jit(solution)/shard_map/all_gather | solution.py:102
  230.6 13.7 %all-to-all-start.2 = ((bf16[768,2,896]{2,0,1:T(8,128)(2,1)}), bf16[768,2,896]{2,0,1:T(8,128)(2,1)}, u32[]{:S(2)}, u32[]{:S(2)}) async-start(bf16[768,2,896]{2,0,1:T(8,128)(2,1)} %bitcast.52), calls=%async_computation.2 | async-start | bytes 5505024 | tf_op jit(solution)/shard_map/all_to_all | solution.py:93
  244.3 14.6 %all-to-all-start.3 = ((bf16[768,2,896]{2,0,1:T(8,128)(2,1)}), bf16[768,2,896]{2,0,1:T(8,128)(2,1)S(1)}, u32[]{:S(2)}, u32[]{:S(2)}) async-start(bf16[768,2,896]{2,0,1:T(8,128)(2,1)} %bitcast.51), calls=%async_computation.3 | async-start | bytes 5505024 | tf_op jit(solution)/shard_map/all_to_all | solution.py:94
  258.9 3.7 %copy-start.3 = (bf16[896,1280]{1,0:T(8,128)(2,1)S(1)}, bf16[896,1280]{1,0:T(8,128)(2,1)}, u32[]{:S(2)}) copy-start(bf16[896,1280]{1,0:T(8,128)(2,1)} %convolution_convert_fusion.1) | copy-start | bytes 6881284
  258.9 3.7 %copy-start.4 = (bf16[896,1280]{1,0:T(8,128)(2,1)S(1)}, bf16[896,1280]{1,0:T(8,128)(2,1)}, u32[]{:S(2)}) copy-start(bf16[896,1280]{1,0:T(8,128)(2,1)} %convolution_convert_fusion.2) | copy-start | bytes 6881284
  262.6 4.0 %copy-start.13 = (bf16[1536,1280]{1,0:T(8,128)(2,1)S(1)}, bf16[1536,1280]{1,0:T(8,128)(2,1)}, u32[]{:S(2)}) copy-start(bf16[1536,1280]{1,0:T(8,128)(2,1)} %all-gather.11.cloned.1.call-done) | copy-start | bytes 11796484
  266.6 2.1 copy-start.11
  268.7 3.5 %copy-start.12 = (bf16[1536,1280]{1,0:T(8,128)(2,1)S(1)}, bf16[1536,1280]{1,0:T(8,128)(2,1)}, u32[]{:S(2)}) copy-start(bf16[1536,1280]{1,0:T(8,128)(2,1)} %all-gather.7.cloned.1.call-done) | copy-start | bytes 11796484
  279.0 15.5 %copy-start.1 = (bf16[64,1792]{1,0:T(8,128)(2,1)S(1)}, bf16[64,1792]{1,0:T(8,128)(2,1)}, u32[]{:S(2)}) copy-start(bf16[64,1792]{1,0:T(8,128)(2,1)} %param.7) | copy-start | bytes 688132
Sparse Core Ops, SparseCore 0:
  13.8 31.7 all-gather.4
  161.8 14.5 all-gather.8
  178.7 17.3 all-gather.6
  198.1 17.3 all-gather.10
where the time goes:
time: 302 us; the launch traced here: 301 us
  blocking collectives  97.5 us (32%)
  matrix products  62.6 us (21%)
  local copies, waits for them, and re-layouts  42.1 us (14%)
  waiting for transfers between devices  38.8 us (13%)
  other arithmetic  26.6 us (9%)
  starting transfers between devices  19.6 us (6%)
  between operations  14 us (5%)
    all_to_all x1, blocking collectives, sent_together(): lax.all_to_all(both, axis, split_axis=split_dim, concat_axis=concat_dim,...  97.5 us
    all_to_all x1, waiting for transfers between devices, shards(): lax.all_to_all(grad_x, 'expert', split_axis=0, concat_axis=0, tiled=True)  37.7 us
    all_to_all x2, local copies, waits for them, and re-layouts, sent_together(): lax.all_to_all(both, axis, split_axis=split_dim, concat_axis=concat_dim,...  19 us
    another operation x1, other arithmetic  9.44 us
    dot_general x2, matrix products, replica_terms(): lax.dot_general(expert_in, grad_up, contract, preferred_element_type=jnp....  8.83 us
    dot_general x1, matrix products, expert_backward(): up_pre = jnp.dot(expert_in, up_mat, preferred_element_type=jnp.float32)  8.82 us
    dot_general x2, matrix products, replica_terms(): lax.dot_general(expert_in, grad_gate, contract, preferred_element_type=jn...  8.68 us
    all_to_all x1, starting transfers between devices, shards(): lax.all_to_all(expert_in, 'dp', split_axis=1, concat_axis=0, tiled=True)  8.62 us
  transfers between devices with their start and end apart: 7, of which 1 were waited for; matrix products, arithmetic and copies ran while one was open for 13% of the time, Pallas kernels for 0%

commit v1 on v0

v1 whole, which is shorter than its diff:
```python
import functools

import jax
import jax.numpy as jnp
from jax import lax
from jax.experimental import pallas as pl
from jax.experimental.pallas import tpu as pltpu
from jax.sharding import PartitionSpec as P

MESH = pl.DeviceIdType.MESH
F32, BF16 = jnp.float32, jnp.bfloat16

TOK, TOP, D, FF = 64, 8, 1792, 1280
HALF = D // 2
CH = 256
CHUNKS = 3
IN_COLS = ((0, 640), (640, 1280), (1280, 1792))
GR_COLS = ((0, 512), (512, 1152), (1152, 1792))
RT_COLS = ((0, 640), (640, 1152), (1152, 1792))
WI = tuple(b - a for a, b in IN_COLS)
WG = tuple(b - a for a, b in GR_COLS)
WR = tuple(b - a for a, b in RT_COLS)
WP = tuple(a + b for a, b in zip(WI, WG))


def expert_of(p, line, j):
    if p == 0:
        return line * 16 + j
    if p == 1:
        return (j // 4) * 16 + line * 4 + j % 4
    return j * 4 + line


def dot(a, b):
    return jnp.dot(a, b, preferred_element_type=F32)


def dot_nt(a, b):
    return lax.dot_general(a, b, (((1,), (1,)), ((), ())), preferred_element_type=F32)


def dot_tn(a, b):
    return lax.dot_general(a, b, (((0,), (0,)), ((), ())), preferred_element_type=F32)


def body(
    ids_ref, comb_ref, tok_ref, gout_ref, wg_ref, wu_ref, wd_ref,
    tg_ref, og_ref, ou_ref, od_ref,
    wfull, line0, line1, line2, mytab, mytabs, tabs, r_tab, c_tab, a_mat, perm,
    spk0, spk1, spk2, rx0, rx1, rx2, xin, gin, hid, gga, gup, gx,
    rs0, rs1, rs2, rr0, rr1, rr2, ls0, ls1, ls2, lr0, lr1, lr2,
    w_loc, w_send, w_recv, lt_send, lt_recv, x_send, x_recv, g_send, g_recv,
    d_send, d_recv, b_send, b_recv, l_send, l_recv, q_send, q_recv, free_sem,
):
    lines, spk, rx = (line0, line1, line2), (spk0, spk1, spk2), (rx0, rx1, rx2)
    rs, rr = (rs0, rs1, rs2), (rr0, rr1, rr2)
    ls, lr = (ls0, ls1, ls2), (lr0, lr1, lr2)
    w_in = (wg_ref, wu_ref, wd_ref)
    w_out = (og_ref, ou_ref, od_ref)
    d = lax.axis_index("dp")
    e = lax.axis_index("expert")
    z, y, x = e // 16, (e // 4) % 4, e % 4
    lcoord = (z, y, x)
    jcoord = (y * 4 + x, z * 4 + x, z * 4 + y)
    partner = (1 - d, e)

    def peer_j(p, i):
        j = jcoord[p]
        return ((j // 4 + i // 4) % 4) * 4 + (j % 4 + i % 4) % 4

    def remote(src, dst, ss, rsem, device):
        return pltpu.make_async_remote_copy(
            src_ref=src, dst_ref=dst, send_sem=ss, recv_sem=rsem,
            device_id=device, device_id_type=MESH,
        )

    barrier = pltpu.get_barrier_semaphore()

    def greet(i, carry):
        for p in range(3):
            pl.semaphore_signal(
                barrier, inc=1,
                device_id=(d, expert_of(p, lcoord[p], peer_j(p, i))), device_id_type=MESH,
            )
        return carry

    lax.fori_loop(1, 16, greet, 0)
    pl.semaphore_signal(barrier, inc=1, device_id=partner, device_id_type=MESH)

    own_rows = pl.ds(pl.multiple_of(d * HALF, HALF), HALF)
    for w in range(3):
        pltpu.make_async_copy(w_in[w].at[0], wfull.at[w, own_rows], w_loc.at[w]).start()

    ids = ids_ref[...].astype(F32)
    e_iota = lax.broadcasted_iota(jnp.int32, (64, TOK), 0).astype(F32)
    named = jnp.zeros((64, TOK), F32)
    for k in range(TOP):
        named = named + jnp.where(ids[k : k + 1, :] == e_iota, 1.0, 0.0)
    upper = (
        lax.broadcasted_iota(jnp.int32, (TOK, TOK), 0)
        < lax.broadcasted_iota(jnp.int32, (TOK, TOK), 1)
    )
    earlier = dot(named.astype(BF16), jnp.where(upper, 1.0, 0.0).astype(BF16))
    mytab[...] = jnp.zeros_like(mytab)
    mytab[0:8, 0:TOK] = ids
    for k in range(TOP):
        mytab[8 + k : 9 + k, 0:TOK] = jnp.sum(
            jnp.where(ids[k : k + 1, :] == e_iota, earlier, 0.0), axis=0, keepdims=True
        )
    mytab[16:24, 0:TOK] = comb_ref[...]
    low = mytab[...]
    high = pltpu.roll(low, 64, 1)
    for p in range(3):
        mytabs[p] = jnp.where(lcoord[p] % 2 == 0, low, high)

    pl.semaphore_wait(barrier, 46)

    for i in range(1, 4):
        for p in range(3):
            to = (d, expert_of(p, (lcoord[p] + i) % 4, jcoord[p]))
            rows = pl.ds(pl.multiple_of(lcoord[p] * TOK, TOK), TOK)
            remote(mytabs.at[p], tabs.at[p, lcoord[p]], lt_send.at[p], lt_recv.at[p], to).start()
            remote(
                tok_ref.at[:, pl.ds(IN_COLS[p][0], WI[p])],
                lines[p].at[rows, pl.ds(0, WI[p])],
                x_send.at[p], x_recv.at[p], to,
            ).start()
            remote(
                gout_ref.at[:, pl.ds(GR_COLS[p][0], WG[p])],
                lines[p].at[rows, pl.ds(WI[p], WG[p])],
                g_send.at[p], g_recv.at[p], to,
            ).start()
    for w in range(3):
        remote(w_in[w].at[0], wfull.at[w, own_rows], w_send.at[w], w_recv.at[w], partner).start()

    for p in range(3):
        rows = pl.ds(pl.multiple_of(lcoord[p] * TOK, TOK), TOK)
        tabs[p, lcoord[p]] = mytabs[p]
        lines[p][rows, 0 : WI[p]] = tok_ref[:, IN_COLS[p][0] : IN_COLS[p][1]]
        lines[p][rows, WI[p] : WP[p]] = gout_ref[:, GR_COLS[p][0] : GR_COLS[p][1]]

    row0 = lax.broadcasted_iota(jnp.int32, (CH, CH), 0)
    col0 = lax.broadcasted_iota(jnp.int32, (CH, CH), 1)
    ry, rxx, rz, rk = (row0 >> 6) & 3, (row0 >> 4) & 3, (row0 >> 2) & 3, row0 & 3
    perm[0] = jnp.where(col0 == (rz << 6) + (rxx << 4) + (ry << 2) + rk, 1.0, 0.0).astype(BF16)
    perm[1] = jnp.where(col0 == (rz << 6) + (ry << 4) + (rxx << 2) + rk, 1.0, 0.0).astype(BF16)

    def line_wait(p):
        remote(tabs.at[p, pl.ds(0, 3)], tabs.at[p, pl.ds(0, 3)], lt_send.at[p], lt_recv.at[p], partner).wait_recv()
        a = lines[p].at[pl.ds(0, 192), pl.ds(0, WI[p])]
        b = lines[p].at[pl.ds(0, 192), pl.ds(WI[p], WG[p])]
        remote(a, a, x_send.at[p], x_recv.at[p], partner).wait_recv()
        remote(b, b, g_send.at[p], g_recv.at[p], partner).wait_recv()

    for p in range(3):
        line_wait(p)
        table = jnp.concatenate([tabs[p, 0] + tabs[p, 1], tabs[p, 2] + tabs[p, 3]], axis=1)
        jj = lax.broadcasted_iota(jnp.int32, (16, 1), 0)
        if p == 0:
            code = jj + lcoord[0] * 16
        elif p == 1:
            code = ((jj >> 2) << 4) + (jj & 3) + lcoord[1] * 4
        else:
            code = (jj << 2) + lcoord[2]
        code = code.astype(F32)
        rank = jnp.zeros((16, CH), F32)
        weight = jnp.zeros((16, CH), F32)
        for k in range(TOP):
            here = table[k : k + 1, :] == code
            rank = rank + jnp.where(here, table[8 + k : 9 + k, :] + 1.0, 0.0)
            weight = weight + jnp.where(here, table[16 + k : 17 + k, :], 0.0)
        r_tab[p] = rank - 1.0
        c_tab[p] = weight

    def pack(c, carry):
        crow = pl.multiple_of(c * CH, CH)
        r_i = lax.broadcasted_iota(jnp.int32, (CH, CH), 0)
        s_i = lax.broadcasted_iota(jnp.int32, (CH, CH), 1) >> 6
        want = jnp.where(((r_i >> 2) & 3) == s_i, (r_i & 3) + 4 * c, -100).astype(F32)
        for p in range(3):
            rank = jnp.broadcast_to(r_tab[p][:, None, :], (16, 16, CH)).reshape(CH, CH)
            wt = jnp.broadcast_to(c_tab[p][:, None, :], (16, 16, CH)).reshape(CH, CH)
            hit = rank == want
            one = jnp.where(hit, 1.0, 0.0).astype(BF16)
            a_mat[p, pl.ds(crow, CH), :] = one
            w_row = jnp.sum(jnp.where(hit, wt, 0.0), axis=1, keepdims=True)
            spk[p][pl.ds(crow, CH), 0 : WI[p]] = dot(one, lines[p][:, 0 : WI[p]]).astype(BF16)
            spk[p][pl.ds(crow, CH), WI[p] : WP[p]] = (
                dot(one, lines[p][:, WI[p] : WP[p]]) * w_row
            ).astype(BF16)

        def send(i, carry2):
            for p in range(3):
                jj = peer_j(p, i)
                to = (d, expert_of(p, lcoord[p], jj))
                remote(
                    spk[p].at[pl.ds(pl.multiple_of(crow + jj * 16, 16), 16)],
                    rx[p].at[pl.ds(pl.multiple_of(crow + jcoord[p] * 16, 16), 16)],
                    d_send.at[p, c], d_recv.at[p, c], to,
                ).start()
            return carry2

        lax.fori_loop(1, 16, send, 0)
        for p in range(3):
            mine = pl.ds(pl.multiple_of(crow + jcoord[p] * 16, 16), 16)
            rx[p][mine, :] = spk[p][mine, :]
        return carry

    lax.fori_loop(0, CHUNKS, pack, 0)

    for w in range(3):
        pltpu.make_async_copy(w_in[w].at[0], wfull.at[w, own_rows], w_loc.at[w]).wait()
        remote(w_in[w].at[0], wfull.at[w, own_rows], w_send.at[w], w_recv.at[w], partner).wait()

    def compute(c, carry):
        crow = pl.multiple_of(c * CH, CH)
        rows = pl.ds(crow, CH)
        for p in range(3):
            part = rx[p].at[pl.ds(0, 240)]
            remote(part, part, d_send.at[p, c], d_recv.at[p, c], partner).wait_recv()
        for p in range(3):
            if p == 0:
                xin[rows, IN_COLS[0][0] : IN_COLS[0][1]] = rx[0][rows, 0 : WI[0]]
                gin[rows, GR_COLS[0][0] : GR_COLS[0][1]] = rx[0][rows, WI[0] : WP[0]]
            else:
                xin[rows, IN_COLS[p][0] : IN_COLS[p][1]] = dot(
                    perm[p - 1], rx[p][rows, 0 : WI[p]]
                ).astype(BF16)
                gin[rows, GR_COLS[p][0] : GR_COLS[p][1]] = dot(
                    perm[p - 1], rx[p][rows, WI[p] : WP[p]]
                ).astype(BF16)

        def units(n, carry2):
            cols = pl.ds(pl.multiple_of(n * 256, 256), 256)
            gate = dot(xin[rows, :], wfull[0, :, cols])
            up = dot(xin[rows, :], wfull[1, :, cols])
            gh = dot(gin[rows, :], wfull[2, :, cols])
            sig = jax.nn.sigmoid(gate)
            act = gate * sig
            hid[rows, cols] = (act * up).astype(BF16)
            gga[rows, cols] = (gh * up * sig * (1.0 + gate * (1.0 - sig))).astype(BF16)
            gup[rows, cols] = (gh * act).astype(BF16)
            return carry2

        lax.fori_loop(0, FF // 256, units, 0)

        def grads(n, carry2):
            cols = pl.ds(pl.multiple_of(n * 256, 256), 256)
            gx[:, cols] = (
                dot_nt(gga[rows, :], wfull[0, cols, :]) + dot_nt(gup[rows, :], wfull[1, cols, :])
            ).astype(BF16)
            return carry2

        lax.fori_loop(0, D // 256, grads, 0)
        for p in range(3):
            cols = gx[:, RT_COLS[p][0] : RT_COLS[p][1]]
            rs[p][rows, :] = cols if p == 0 else dot_tn(perm[p - 1], cols).astype(BF16)

        def send(i, carry2):
            for p in range(3):
                jj = peer_j(p, i)
                to = (d, expert_of(p, lcoord[p], jj))
                remote(
                    rs[p].at[pl.ds(pl.multiple_of(crow + jj * 16, 16), 16)],
                    rr[p].at[pl.ds(pl.multiple_of(crow + jcoord[p] * 16, 16), 16)],
                    b_send.at[p, c], b_recv.at[p, c], to,
                ).start()
            return carry2

        lax.fori_loop(1, 16, send, 0)
        for p in range(3):
            mine = pl.ds(pl.multiple_of(crow + jcoord[p] * 16, 16), 16)
            rr[p][mine, :] = rs[p][mine, :]
        return carry

    lax.fori_loop(0, CHUNKS, compute, 0)
    pl.semaphore_signal(free_sem, inc=1, device_id=partner, device_id_type=MESH)

    far = (1 - d) * HALF
    near = d * HALF

    def far_terms(n, carry):
        cols = pl.ds(pl.multiple_of(n * 256, 256), 256)
        half = pl.ds(pl.multiple_of(far, 128), HALF)
        wfull[0, 0:HALF, cols] = dot_tn(xin[:, half], gga[:, cols]).astype(BF16)
        wfull[1, 0:HALF, cols] = dot_tn(xin[:, half], gup[:, cols]).astype(BF16)
        wfull[2, 0:HALF, cols] = dot_tn(gin[:, half], hid[:, cols]).astype(BF16)
        for w in range(3):
            remote(
                wfull.at[w, pl.ds(0, HALF), cols], wfull.at[w, pl.ds(HALF, HALF), cols],
                q_send.at[n], q_recv.at[n], partner,
            ).start()
        return carry

    pl.semaphore_wait(free_sem, 1)
    lax.fori_loop(0, FF // 256, far_terms, 0)

    for p in range(3):
        for c in range(CHUNKS):
            part = rr[p].at[pl.ds(0, 240)]
            remote(part, part, b_send.at[p, c], b_recv.at[p, c], partner).wait_recv()
        ls[p][...] = dot_tn(a_mat[p], rr[p][...]).astype(BF16)
        for i in range(1, 4):
            s = (lcoord[p] + i) % 4
            to = (d, expert_of(p, s, jcoord[p]))
            remote(
                ls[p].at[pl.ds(pl.multiple_of(s * TOK, TOK), TOK)],
                lr[p].at[lcoord[p]],
                l_send.at[p], l_recv.at[p], to,
            ).start()
        lr[p][lcoord[p]] = ls[p][pl.ds(pl.multiple_of(lcoord[p] * TOK, TOK), TOK), :]

    def near_terms(n, carry):
        cols = pl.ds(pl.multiple_of(n * 256, 256), 256)
        half = pl.ds(pl.multiple_of(near, 128), HALF)
        terms = (
            dot_tn(xin[:, half], gga[:, cols]),
            dot_tn(xin[:, half], gup[:, cols]),
            dot_tn(gin[:, half], hid[:, cols]),
        )
        part = wfull.at[pl.ds(0, 3), pl.ds(HALF, HALF), cols]
        remote(part, part, q_send.at[n], q_recv.at[n], partner).wait_recv()
        for w in range(3):
            other = wfull[w, HALF:D, cols].astype(F32)
            w_out[w][0, :, cols] = (terms[w].astype(BF16).astype(F32) + other).astype(BF16)
        return carry

    lax.fori_loop(0, FF // 256, near_terms, 0)

    for p in range(3):
        part = lr[p].at[pl.ds(0, 3)]
        remote(part, part, l_send.at[p], l_recv.at[p], partner).wait_recv()
        total = lr[p][0].astype(F32) + lr[p][1].astype(F32)
        total = total + lr[p][2].astype(F32) + lr[p][3].astype(F32)
        tg_ref[:, RT_COLS[p][0] : RT_COLS[p][1]] = total.astype(BF16)

    for p in range(3):
        remote(tabs.at[p, pl.ds(0, 3)], tabs.at[p, pl.ds(0, 3)], lt_send.at[p], lt_recv.at[p], partner).wait_send()
        a = lines[p].at[pl.ds(0, 192), pl.ds(0, WI[p])]
        b = lines[p].at[pl.ds(0, 192), pl.ds(WI[p], WG[p])]
        remote(a, a, x_send.at[p], x_recv.at[p], partner).wait_send()
        remote(b, b, g_send.at[p], g_recv.at[p], partner).wait_send()
        for c in range(CHUNKS):
            part = rx[p].at[pl.ds(0, 240)]
            remote(part, part, d_send.at[p, c], d_recv.at[p, c], partner).wait_send()
            part = rr[p].at[pl.ds(0, 240)]
            remote(part, part, b_send.at[p, c], b_recv.at[p, c], partner).wait_send()
        part = lr[p].at[pl.ds(0, 3)]
        remote(part, part, l_send.at[p], l_recv.at[p], partner).wait_send()
    for n in range(FF // 256):
        part = wfull.at[pl.ds(0, 3), pl.ds(0, HALF), pl.ds(n * 256, 256)]
        remote(part, part, q_send.at[n], q_recv.at[n], partner).wait_send()


def shards(tokens, grad_out, combine, expert_ids, w_gate, w_up, w_down):
    vm, hbm = pl.BlockSpec(memory_space=pltpu.VMEM), pl.BlockSpec(memory_space=pl.ANY)
    rows = CHUNKS * CH
    v = pltpu.VMEM
    scratch = [
        v((3, D, FF), BF16),
        *[v((CH, w), BF16) for w in WP],
        v((24, 128), F32), v((3, 24, 128), F32), v((3, 4, 24, 128), F32),
        v((3, 16, CH), F32), v((3, 16, CH), F32),
        v((3, rows, CH), BF16), v((2, CH, CH), BF16),
        *[v((rows, w), BF16) for w in WP],
        *[v((rows, w), BF16) for w in WP],
        v((rows, D), BF16), v((rows, D), BF16),
        v((rows, FF), BF16), v((rows, FF), BF16), v((rows, FF), BF16),
        v((CH, D), BF16),
        *[v((rows, w), BF16) for w in WR],
        *[v((rows, w), BF16) for w in WR],
        *[v((CH, w), BF16) for w in WR],
        *[v((4, TOK, w), BF16) for w in WR],
    ]
    dma = pltpu.SemaphoreType.DMA
    sems = [
        *[dma((3,))] * 9,
        *[dma((3, 3))] * 4,
        *[dma((3,))] * 2,
        *[dma((FF // 256,))] * 2,
        pltpu.SemaphoreType.REGULAR,
    ]
    wshape = jax.ShapeDtypeStruct((1, HALF, FF), BF16)
    return pl.pallas_call(
        body,
        out_shape=(jax.ShapeDtypeStruct((TOK, D), BF16), wshape, wshape, wshape),
        in_specs=[vm, vm, vm, vm, hbm, hbm, hbm],
        out_specs=(vm, vm, vm, vm),
        scratch_shapes=scratch + sems,
        compiler_params=pltpu.CompilerParams(
            collective_id=0, has_side_effects=True, vmem_limit_bytes=67043328
        ),
        name="routed_backward",
    )(expert_ids.T, combine.T, tokens, grad_out, w_gate, w_up, w_down)


def solution(mesh):
    rows = P(("dp", "expert"), None)
    weights = P("expert", "dp", None)
    return jax.shard_map(
        shards,
        mesh=mesh,
        in_specs=(rows, rows, rows, rows, weights, weights, weights),
        out_specs=(rows, weights, weights, weights),
        check_vma=False,
    )
```

time: 302 us -> 112 us (0.37)
  Pallas kernels: 0 us -> 102 us
  blocking collectives: 97.5 us -> 0 us
  matrix products: 62.6 us -> 0 us
  waiting for transfers between devices: 38.8 us -> 0 us
  local copies, waits for them, and re-layouts: 42.1 us -> 8.83 us
  other arithmetic: 26.6 us -> 0 us
  starting transfers between devices: 19.6 us -> 0 us
  between operations: 14 us -> 0.64 us
    pallas_call x0 -> x1, Pallas kernels: none -> 102 us  [shards(): pl.pallas_call(body, out_shape=(jax.ShapeDtypeStruct((TOK, D), BF16), wsh...]
    all_to_all x1 -> x0, blocking collectives: 97.5 us -> none  [sent_together(): lax.all_to_all(both, axis, split_axis=split_dim, concat_axis=concat_dim,...]
    dot_general x15 -> x0, matrix products: 62.6 us -> none  [the longest x2 8.83 us: replica_terms(): lax.dot_general(expert_in, grad_up, contract, preferred_element_type=jnp....]
    all_to_all x3 -> x0, waiting for transfers between devices: 37.7 us -> none  [the longest x1 37.7 us: shards(): lax.all_to_all(grad_x, 'expert', split_axis=0, concat_axis=0, tiled=True)]
    all_to_all x6 -> x0, local copies, waits for them, and re-layouts: 28.8 us -> none  [the longest x2 19 us: sent_together(): lax.all_to_all(both, axis, split_axis=split_dim, concat_axis=concat_dim,...]
    all_to_all x3 -> x0, starting transfers between devices: 19.2 us -> none  [the longest x1 8.62 us: shards(): lax.all_to_all(expert_in, 'dp', split_axis=1, concat_axis=0, tiled=True)]
    concatenate x4 -> x0, other arithmetic: 16.2 us -> none  [the longest x2 6.96 us: replica_terms(): jnp.concatenate([lax.dot_general(expert_in, grad_gate, contract, preferre...]
    another operation x1 -> x0, other arithmetic: 9.44 us -> none
  transfers between devices with their start and end apart: 7 -> 0, of which waited for: 1 -> 0; matrix products, arithmetic and copies ran while one was open for 13% -> 0% of each run, Pallas kernels for 0% -> 0%
where the time goes in v1:
time: 112 us
  Pallas kernels  102 us (91%)
  local copies, waits for them, and re-layouts  8.83 us (8%)
    pallas_call x1, Pallas kernels, shards(): pl.pallas_call(body, out_shape=(jax.ShapeDtypeStruct((TOK, D), BF16), wsh...  102 us
    unnamed x8, local copies, waits for them, and re-layouts  8.83 us

profile of v1, /device:TPU:1, one launch (start us, length us, event | category | flops | bytes accessed | tf_op | source)
XLA Modules:
  0.0 111.7 jit_solution(7662122302814296191)
XLA Ops:
  0.6 102.3 %routed_backward.1 = (bf16[64,1792]{1,0:T(8,128)(2,1)}, bf16[1,896,1280]{2,1,0:T(8,128)(2,1)}, bf16[1,896,1280]{2,1,0:T(8,128)(2,1)}, bf16[1,896,1280]{2,1,0:T(8,128)(2,1)}) custom-call(s32[8,64]{1,0:T(8,128)} %bitcast.2, f32[8,64]{1,0:T(8,128)} %bitcast.3, bf16[64,1792]{1,0:T(8,128)(2,1)} %tok_ref.1, bf16[64,1792]{1,0:T(8,128)(2,1)} %gout_ref.1, ...), custom_call_target="tpu_custom_call" | custom-call | tf_op jit(solution)/shard_map/routed_backward/pallas_call | solution.py:384
  102.9 1.6 %copy.15 = bf16[64,1792]{1,0:T(8,128)(2,1)} copy(bf16[64,1792]{1,0:T(8,128)(2,1)} %get-tuple-element.8) | data formatting | bytes 458752
  104.6 0.0 copy-start.1
  104.6 3.3 %copy.16 = bf16[1,896,1280]{2,1,0:T(8,128)(2,1)} copy(bf16[1,896,1280]{2,1,0:T(8,128)(2,1)} %get-tuple-element.9) | data formatting | bytes 4587520
  107.9 0.0 copy-done.1
  107.9 0.0 copy-start
  107.9 1.4 %copy.17 = bf16[1,896,1280]{2,1,0:T(8,128)(2,1)} copy(bf16[1,896,1280]{2,1,0:T(8,128)(2,1)S(1)} %copy-done.1) | data formatting | bytes 4587520
  109.3 1.1 copy-done
  110.4 1.4 %copy.18 = bf16[1,896,1280]{2,1,0:T(8,128)(2,1)} copy(bf16[1,896,1280]{2,1,0:T(8,128)(2,1)S(1)} %copy-done) | data formatting | bytes 4587520
Async XLA Ops:
  104.6 3.3 %copy-start.1 = (bf16[1,896,1280]{2,1,0:T(8,128)(2,1)S(1)}, bf16[1,896,1280]{2,1,0:T(8,128)(2,1)}, u32[]{:S(2)}) copy-start(bf16[1,896,1280]{2,1,0:T(8,128)(2,1)} %get-tuple-element.10) | copy-start | bytes 6881284
  107.9 2.5 %copy-start = (bf16[1,896,1280]{2,1,0:T(8,128)(2,1)S(1)}, bf16[1,896,1280]{2,1,0:T(8,128)(2,1)}, u32[]{:S(2)}) copy-start(bf16[1,896,1280]{2,1,0:T(8,128)(2,1)} %get-tuple-element.11) | copy-start | bytes 6881284

commit v2 on v1

v2 whole, which is shorter than its diff:
```python
import functools

import jax
import jax.numpy as jnp
from jax import lax
from jax.experimental import pallas as pl
from jax.experimental.pallas import tpu as pltpu
from jax.sharding import PartitionSpec as P

MESH = pl.DeviceIdType.MESH
F32, BF16 = jnp.float32, jnp.bfloat16

TOK, TOP, D, FF = 64, 8, 1792, 1280
HALF = D // 2
CH = 256
CHUNKS = 3
TILES = FF // 256
IN_COLS = ((0, 640), (640, 1280), (1280, 1792))
GR_COLS = ((0, 512), (512, 1152), (1152, 1792))
RT_COLS = ((0, 640), (640, 1152), (1152, 1792))
WI = tuple(b - a for a, b in IN_COLS)
WG = tuple(b - a for a, b in GR_COLS)
WR = tuple(b - a for a, b in RT_COLS)
WP = tuple(a + b for a, b in zip(WI, WG))


def expert_of(p, line, j):
    if p == 0:
        return line * 16 + j
    if p == 1:
        return (j // 4) * 16 + line * 4 + j % 4
    return j * 4 + line


def dot(a, b):
    return jnp.dot(a, b, preferred_element_type=F32)


def dot_nt(a, b):
    return lax.dot_general(a, b, (((1,), (1,)), ((), ())), preferred_element_type=F32)


def dot_tn(a, b):
    return lax.dot_general(a, b, (((0,), (0,)), ((), ())), preferred_element_type=F32)


def body(
    ids_hbm, comb_hbm, tok_hbm, gout_hbm, wg_ref, wu_ref, wd_ref,
    tg_ref, og_ref, ou_ref, od_ref,
    ids_ref, comb_ref, tok_ref, gout_ref, wfull, line0, line1, line2, mytab, mytabs, tabs, r_tab, c_tab, a_mat, perm,
    spk0, spk1, spk2, rx0, rx1, rx2, xg, hg, far_xg, far_hg, gx,
    rr0, rr1, rr2, lr0, lr1, lr2,
    i_loc, w_loc, w_send, w_recv, lt_send, lt_recv, x_send, x_recv, g_send, g_recv,
    d_send, d_recv, b_send, b_recv, l_send, l_recv, q_send, q_recv, h_send, h_recv,
):
    lines, spk, rx = (line0, line1, line2), (spk0, spk1, spk2), (rx0, rx1, rx2)
    rr = (rr0, rr1, rr2)
    lr = (lr0, lr1, lr2)
    w_in = (wg_ref, wu_ref, wd_ref)
    w_out = (og_ref, ou_ref, od_ref)
    d = lax.axis_index("dp")
    e = lax.axis_index("expert")
    z, y, x = e // 16, (e // 4) % 4, e % 4
    lcoord = (z, y, x)
    jcoord = (y * 4 + x, z * 4 + x, z * 4 + y)
    partner = (1 - d, e)

    def peer_j(p, i):
        j = jcoord[p]
        return ((j // 4 + i // 4) % 4) * 4 + (j % 4 + i % 4) % 4

    def remote(src, dst, ss, rsem, device):
        return pltpu.make_async_remote_copy(
            src_ref=src, dst_ref=dst, send_sem=ss, recv_sem=rsem,
            device_id=device, device_id_type=MESH,
        )

    small = ((ids_hbm, ids_ref), (comb_hbm, comb_ref), (tok_hbm, tok_ref), (gout_hbm, gout_ref))
    for k, (src, dst) in enumerate(small):
        pltpu.make_async_copy(src, dst, i_loc.at[k]).start()

    barrier = pltpu.get_barrier_semaphore()

    def greet(p, i):
        pl.semaphore_signal(
            barrier, inc=1,
            device_id=(d, expert_of(p, lcoord[p], peer_j(p, i))), device_id_type=MESH,
        )

    for i in range(1, 16):
        greet(0, i)
        if i >= 4:
            greet(1, i)
            if i % 4:
                greet(2, i)
    pl.semaphore_signal(barrier, inc=1, device_id=partner, device_id_type=MESH)

    own_rows = pl.ds(pl.multiple_of(d * HALF, HALF), HALF)
    for w in range(3):
        pltpu.make_async_copy(w_in[w].at[0], wfull.at[w, own_rows], w_loc.at[w]).start()

    for k, (src, dst) in enumerate(small):
        pltpu.make_async_copy(src, dst, i_loc.at[k]).wait()
    ids = ids_ref[...].astype(F32)
    e_iota = lax.broadcasted_iota(jnp.int32, (64, TOK), 0).astype(F32)
    named = jnp.zeros((64, TOK), F32)
    for k in range(TOP):
        named = named + jnp.where(ids[k : k + 1, :] == e_iota, 1.0, 0.0)
    upper = (
        lax.broadcasted_iota(jnp.int32, (TOK, TOK), 0)
        < lax.broadcasted_iota(jnp.int32, (TOK, TOK), 1)
    )
    earlier = dot(named.astype(BF16), jnp.where(upper, 1.0, 0.0).astype(BF16))
    mytab[...] = jnp.zeros_like(mytab)
    mytab[0:8, 0:TOK] = ids
    for k in range(TOP):
        mytab[8 + k : 9 + k, 0:TOK] = jnp.sum(
            jnp.where(ids[k : k + 1, :] == e_iota, earlier, 0.0), axis=0, keepdims=True
        )
    mytab[16:24, 0:TOK] = comb_ref[...]
    low = mytab[...]
    high = pltpu.roll(low, 64, 1)
    for p in range(3):
        mytabs[p] = jnp.where(lcoord[p] % 2 == 0, low, high)

    pl.semaphore_wait(barrier, 37)

    for i in range(1, 4):
        for p in range(3):
            to = (d, expert_of(p, (lcoord[p] + i) % 4, jcoord[p]))
            rows = pl.ds(pl.multiple_of(lcoord[p] * TOK, TOK), TOK)
            remote(mytabs.at[p], tabs.at[p, lcoord[p]], lt_send.at[p], lt_recv.at[p], to).start()
            remote(
                tok_ref.at[:, pl.ds(IN_COLS[p][0], WI[p])],
                lines[p].at[rows, pl.ds(0, WI[p])],
                x_send.at[p], x_recv.at[p], to,
            ).start()
            remote(
                gout_ref.at[:, pl.ds(GR_COLS[p][0], WG[p])],
                lines[p].at[rows, pl.ds(WI[p], WG[p])],
                g_send.at[p], g_recv.at[p], to,
            ).start()
    for w in range(3):
        remote(w_in[w].at[0], wfull.at[w, own_rows], w_send.at[w], w_recv.at[w], partner).start()

    for p in range(3):
        rows = pl.ds(pl.multiple_of(lcoord[p] * TOK, TOK), TOK)
        tabs[p, lcoord[p]] = mytabs[p]
        lines[p][rows, 0 : WI[p]] = tok_ref[:, IN_COLS[p][0] : IN_COLS[p][1]]
        lines[p][rows, WI[p] : WP[p]] = gout_ref[:, GR_COLS[p][0] : GR_COLS[p][1]]

    row0 = lax.broadcasted_iota(jnp.int32, (CH, CH), 0)
    col0 = lax.broadcasted_iota(jnp.int32, (CH, CH), 1)
    ry, rxx, rz, rk = (row0 >> 6) & 3, (row0 >> 4) & 3, (row0 >> 2) & 3, row0 & 3
    perm[0] = jnp.where(col0 == (rz << 6) + (rxx << 4) + (ry << 2) + rk, 1.0, 0.0).astype(BF16)
    perm[1] = jnp.where(col0 == (rz << 6) + (ry << 4) + (rxx << 2) + rk, 1.0, 0.0).astype(BF16)
    perm[2] = jnp.where(col0 == row0, 1.0, 0.0).astype(BF16)
    perm[3] = jnp.where(col0 == (rxx << 6) + (rz << 4) + (ry << 2) + rk, 1.0, 0.0).astype(BF16)

    def line_wait(p):
        remote(tabs.at[p, pl.ds(0, 3)], tabs.at[p, pl.ds(0, 3)], lt_send.at[p], lt_recv.at[p], partner).wait_recv()
        a = lines[p].at[pl.ds(0, 192), pl.ds(0, WI[p])]
        b = lines[p].at[pl.ds(0, 192), pl.ds(WI[p], WG[p])]
        remote(a, a, x_send.at[p], x_recv.at[p], partner).wait_recv()
        remote(b, b, g_send.at[p], g_recv.at[p], partner).wait_recv()

    for p in range(3):
        line_wait(p)
        table = jnp.concatenate([tabs[p, 0] + tabs[p, 1], tabs[p, 2] + tabs[p, 3]], axis=1)
        jj = lax.broadcasted_iota(jnp.int32, (16, 1), 0)
        if p == 0:
            code = jj + lcoord[0] * 16
        elif p == 1:
            code = ((jj >> 2) << 4) + (jj & 3) + lcoord[1] * 4
        else:
            code = (jj << 2) + lcoord[2]
        code = code.astype(F32)
        rank = jnp.zeros((16, CH), F32)
        weight = jnp.zeros((16, CH), F32)
        for k in range(TOP):
            here = table[k : k + 1, :] == code
            rank = rank + jnp.where(here, table[8 + k : 9 + k, :] + 1.0, 0.0)
            weight = weight + jnp.where(here, table[16 + k : 17 + k, :], 0.0)
        r_tab[p] = rank - 1.0
        c_tab[p] = weight

    def dispatch(c):
        crow = c * CH

        def send(i, carry2):
            for p in range(3):
                jj = peer_j(p, i)
                to = (d, expert_of(p, lcoord[p], jj))
                remote(
                    spk[p].at[pl.ds(pl.multiple_of(crow + jj * 16, 16), 16)],
                    rx[p].at[pl.ds(pl.multiple_of(crow + jcoord[p] * 16, 16), 16)],
                    d_send.at[p, c], d_recv.at[p, c], to,
                ).start()
            return carry2

        lax.fori_loop(1, 16, send, 0)
        for p in range(3):
            mine = pl.ds(pl.multiple_of(crow + jcoord[p] * 16, 16), 16)
            rx[p][mine, :] = spk[p][mine, :]

    def give_back(c):
        crow = c * CH

        def send(i, carry2):
            for p in range(3):
                jj = peer_j(p, i)
                to = (d, expert_of(p, lcoord[p], jj))
                remote(
                    spk[p].at[pl.ds(pl.multiple_of(crow + jj * 16, 16), 16), pl.ds(0, WR[p])],
                    rr[p].at[pl.ds(pl.multiple_of(crow + jcoord[p] * 16, 16), 16)],
                    b_send.at[p, c], b_recv.at[p, c], to,
                ).start()
            return carry2

        lax.fori_loop(1, 16, send, 0)
        for p in range(3):
            mine = pl.ds(pl.multiple_of(crow + jcoord[p] * 16, 16), 16)
            rr[p][mine, :] = spk[p][mine, 0 : WR[p]]

    def pack(c, carry):
        crow = pl.multiple_of(c * CH, CH)
        r_i = lax.broadcasted_iota(jnp.int32, (CH, CH), 0)
        s_i = lax.broadcasted_iota(jnp.int32, (CH, CH), 1) >> 6
        want = jnp.where(((r_i >> 2) & 3) == s_i, (r_i & 3) + 4 * c, -100).astype(F32)
        for p in range(3):
            rank = jnp.broadcast_to(r_tab[p][:, None, :], (16, 16, CH)).reshape(CH, CH)
            wt = jnp.broadcast_to(c_tab[p][:, None, :], (16, 16, CH)).reshape(CH, CH)
            hit = rank == want
            one = jnp.where(hit, 1.0, 0.0).astype(BF16)
            a_mat[p, pl.ds(crow, CH), :] = one
            w_row = jnp.sum(jnp.where(hit, wt, 0.0), axis=1, keepdims=True)
            spk[p][pl.ds(crow, CH), 0 : WI[p]] = dot(one, lines[p][:, 0 : WI[p]]).astype(BF16)
            spk[p][pl.ds(crow, CH), WI[p] : WP[p]] = (
                dot(one, lines[p][:, WI[p] : WP[p]]) * w_row
            ).astype(BF16)

        @pl.when(c < 2)
        def _():
            dispatch(c)

        return carry

    lax.fori_loop(0, CHUNKS, pack, 0)

    def clear(n, carry):
        rows = pl.ds(pl.multiple_of(n * 128, 128), 128)
        for w in range(3):
            w_out[w][0, rows, :] = jnp.zeros((128, FF), F32)
        return carry

    lax.fori_loop(0, HALF // 128, clear, 0)

    for w in range(3):
        pltpu.make_async_copy(w_in[w].at[0], wfull.at[w, own_rows], w_loc.at[w]).wait()
        remote(w_in[w].at[0], wfull.at[w, own_rows], w_send.at[w], w_recv.at[w], partner).wait()

    near = pl.ds(pl.multiple_of(d * HALF, 128), HALF)
    far = pl.ds(pl.multiple_of((1 - d) * HALF, 128), HALF)

    def far_wait(c):
        remote(far_xg.at[c], far_xg.at[c], q_send.at[c], q_recv.at[c], partner).wait_recv()
        remote(far_hg.at[c], far_hg.at[c], h_send.at[c], h_recv.at[c], partner).wait_recv()

    def terms(c, n, carry):
        b = c % 2
        cols = pl.ds(pl.multiple_of(n * 256, 256), 256)
        for w in range(3):
            k = w // 2
            w_out[w][0, :, cols] += dot_tn(xg[b, k, :, near], hg[b, w, :, cols]) + dot_tn(
                far_xg[c, k], far_hg[c, w, :, cols]
            )
        return carry

    def compute(c, carry):
        crow = pl.multiple_of(c * CH, CH)
        rows = pl.ds(crow, CH)
        b = c % 2

        @pl.when(c >= 2)
        def _():
            remote(far_xg.at[c - 2], far_xg.at[c - 2], q_send.at[c - 2], q_recv.at[c - 2], partner).wait_send()
            remote(far_hg.at[c - 2], far_hg.at[c - 2], h_send.at[c - 2], h_recv.at[c - 2], partner).wait_send()

        for p in range(3):
            part = rx[p].at[pl.ds(0, 240)]
            remote(part, part, d_send.at[p, c], d_recv.at[p, c], partner).wait_recv()

        @pl.when(c >= 1)
        def _():
            give_back(c - 1)

        for p in range(3):
            i0, i1 = IN_COLS[p]
            g0, g1 = GR_COLS[p]
            if p == 0:
                xg[b, 0, :, i0:i1] = rx[0][rows, 0 : WI[0]]
                xg[b, 1, :, g0:g1] = rx[0][rows, WI[0] : WP[0]]
            else:
                xg[b, 0, :, i0:i1] = dot(perm[p - 1], rx[p][rows, 0 : WI[p]]).astype(BF16)
                xg[b, 1, :, g0:g1] = dot(perm[p - 1], rx[p][rows, WI[p] : WP[p]]).astype(BF16)
        for k in range(2):
            remote(
                xg.at[b, k, :, far], far_xg.at[c, k], q_send.at[c], q_recv.at[c], partner
            ).start()

        def units(n, carry2):
            cols = pl.ds(pl.multiple_of(n * 256, 256), 256)
            gate = dot(xg[b, 0], wfull[0, :, cols])
            up = dot(xg[b, 0], wfull[1, :, cols])
            gh = dot(xg[b, 1], wfull[2, :, cols])
            sig = jax.nn.sigmoid(gate)
            act = gate * sig
            hg[b, 2, :, cols] = (act * up).astype(BF16)
            hg[b, 0, :, cols] = (gh * up * sig * (1.0 + gate * (1.0 - sig))).astype(BF16)
            hg[b, 1, :, cols] = (gh * act).astype(BF16)
            return carry2

        lax.fori_loop(0, TILES, units, 0)

        @pl.when(c == 0)
        def _():
            dispatch(2)

        for k in range(3):
            remote(hg.at[b, k], far_hg.at[c, k], h_send.at[c], h_recv.at[c], partner).start()

        def grads(n, carry2):
            cols = pl.ds(pl.multiple_of(n * 256, 256), 256)
            gx[cols, :] = (
                dot_nt(wfull[0, cols, :], hg[b, 0]) + dot_nt(wfull[1, cols, :], hg[b, 1])
            ).astype(BF16)
            return carry2

        lax.fori_loop(0, D // 256, grads, 0)
        for p in range(3):
            part = rx[p].at[pl.ds(0, 240)]
            remote(part, part, d_send.at[p, c], d_recv.at[p, c], partner).wait_send()
            back = perm[(2, 0, 3)[p]]
            spk[p][rows, 0 : WR[p]] = dot_nt(back, gx[RT_COLS[p][0] : RT_COLS[p][1], :]).astype(BF16)

        @pl.when(c == 0)
        def _():
            far_wait(c)
            lax.fori_loop(0, TILES, functools.partial(terms, c), 0)

        return carry

    lax.fori_loop(0, CHUNKS, compute, 0)
    give_back(CHUNKS - 1)
    far_wait(1)
    far_wait(2)

    def late_terms(i, carry):
        return terms(1 + i // TILES, i % TILES, carry)

    lax.fori_loop(0, TILES + 2, late_terms, 0)

    for p in range(3):
        for c in range(CHUNKS):
            part = rr[p].at[pl.ds(0, 240)]
            remote(part, part, b_send.at[p, c], b_recv.at[p, c], partner).wait_recv()
        lines[p][:, 0 : WR[p]] = dot_tn(a_mat[p], rr[p][...]).astype(BF16)
        for i in range(1, 4):
            s = (lcoord[p] + i) % 4
            to = (d, expert_of(p, s, jcoord[p]))
            remote(
                lines[p].at[pl.ds(pl.multiple_of(s * TOK, TOK), TOK), pl.ds(0, WR[p])],
                lr[p].at[lcoord[p]],
                l_send.at[p], l_recv.at[p], to,
            ).start()
        lr[p][lcoord[p]] = lines[p][
            pl.ds(pl.multiple_of(lcoord[p] * TOK, TOK), TOK), 0 : WR[p]
        ]

    lax.fori_loop(TILES + 2, 2 * TILES, late_terms, 0)

    for p in range(3):
        part = lr[p].at[pl.ds(0, 3)]
        remote(part, part, l_send.at[p], l_recv.at[p], partner).wait_recv()
        total = lr[p][0].astype(F32) + lr[p][1].astype(F32)
        total = total + lr[p][2].astype(F32) + lr[p][3].astype(F32)
        tg_ref[:, RT_COLS[p][0] : RT_COLS[p][1]] = total.astype(BF16)

    for p in range(3):
        remote(tabs.at[p, pl.ds(0, 3)], tabs.at[p, pl.ds(0, 3)], lt_send.at[p], lt_recv.at[p], partner).wait_send()
        a = lines[p].at[pl.ds(0, 192), pl.ds(0, WI[p])]
        b = lines[p].at[pl.ds(0, 192), pl.ds(WI[p], WG[p])]
        remote(a, a, x_send.at[p], x_recv.at[p], partner).wait_send()
        remote(b, b, g_send.at[p], g_recv.at[p], partner).wait_send()
        for c in range(CHUNKS):
            part = rr[p].at[pl.ds(0, 240)]
            remote(part, part, b_send.at[p, c], b_recv.at[p, c], partner).wait_send()
        part = lr[p].at[pl.ds(0, 3)]
        remote(part, part, l_send.at[p], l_recv.at[p], partner).wait_send()
    for c in range(1, CHUNKS):
        remote(far_xg.at[c], far_xg.at[c], q_send.at[c], q_recv.at[c], partner).wait_send()
        remote(far_hg.at[c], far_hg.at[c], h_send.at[c], h_recv.at[c], partner).wait_send()


def shards(tokens, grad_out, combine, expert_ids, w_gate, w_up, w_down):
    vm, hbm = pl.BlockSpec(memory_space=pltpu.VMEM), pl.BlockSpec(memory_space=pl.ANY)
    rows = CHUNKS * CH
    v = pltpu.VMEM
    scratch = [
        v((TOP, TOK), jnp.int32), v((TOP, TOK), F32), v((TOK, D), BF16), v((TOK, D), BF16),
        v((3, D, FF), BF16),
        *[v((CH, w), BF16) for w in WP],
        v((24, 128), F32), v((3, 24, 128), F32), v((3, 4, 24, 128), F32),
        v((3, 16, CH), F32), v((3, 16, CH), F32),
        v((3, rows, CH), BF16), v((4, CH, CH), BF16),
        *[v((rows, w), BF16) for w in WP],
        *[v((rows, w), BF16) for w in WP],
        v((2, 2, CH, D), BF16), v((2, 3, CH, FF), BF16),
        v((CHUNKS, 2, CH, HALF), BF16), v((CHUNKS, 3, CH, FF), BF16),
        v((D, CH), BF16),
        *[v((rows, w), BF16) for w in WR],
        *[v((4, TOK, w), BF16) for w in WR],
    ]
    dma = pltpu.SemaphoreType.DMA
    sems = [
        dma((4,)),
        *[dma((3,))] * 9,
        *[dma((3, 3))] * 4,
        *[dma((3,))] * 6,
    ]
    sums = v((1, HALF, FF), F32)
    token_grad, *grads = pl.pallas_call(
        body,
        out_shape=(v((TOK, D), BF16), sums, sums, sums),
        in_specs=[hbm] * 7,
        out_specs=(vm, vm, vm, vm),
        scratch_shapes=scratch + sems,
        compiler_params=pltpu.CompilerParams(
            collective_id=0, has_side_effects=True, vmem_limit_bytes=52500000
        ),
        name="routed_backward",
    )(expert_ids.T, combine.T, tokens, grad_out, w_gate, w_up, w_down)
    return (token_grad, *[g.astype(BF16) for g in grads])


def solution(mesh):
    rows = P(("dp", "expert"), None)
    weights = P("expert", "dp", None)
    return jax.shard_map(
        shards,
        mesh=mesh,
        in_specs=(rows, rows, rows, rows, weights, weights, weights),
        out_specs=(rows, weights, weights, weights),
        check_vma=False,
    )
```

time: 112 us -> 102 us (0.911)
  local copies, waits for them, and re-layouts: 8.83 us -> 0.69 us
  Pallas kernels: 102 us -> 94.9 us
  other arithmetic: 0 us -> 4.82 us
    unnamed x8 -> x1, local copies, waits for them, and re-layouts: 8.83 us -> 0.69 us
    pallas_call x1, Pallas kernels: 102 us -> 94.9 us  [shards(): pl.pallas_call(body, out_shape=(v((TOK, D), BF16), sums, sums, sums), in_...]
    convert_element_type x0 -> x3, other arithmetic: none -> 4.82 us  [shards(): return (token_grad, *[g.astype(BF16) for g in grads])]
where the time goes in v2:
time: 102 us; the launch traced here: 101 us
  Pallas kernels  94.9 us (93%)
  other arithmetic  4.82 us (5%)
    pallas_call x1, Pallas kernels, shards(): pl.pallas_call(body, out_shape=(v((TOK, D), BF16), sums, sums, sums), in_...  94.9 us
    convert_element_type x3, other arithmetic, shards(): return (token_grad, *[g.astype(BF16) for g in grads])  4.82 us

profile of v2, /device:TPU:1, one launch (start us, length us, event | category | flops | bytes accessed | tf_op | source)
XLA Modules:
  0.0 101.1 jit_solution(5582131645674689085)
XLA Ops:
  0.6 94.9 %routed_backward.1 = (bf16[64,1792]{1,0:T(8,128)(2,1)S(1)}, f32[1,896,1280]{2,1,0:T(8,128)S(1)}, f32[1,896,1280]{2,1,0:T(8,128)S(1)}, f32[1,896,1280]{2,1,0:T(8,128)S(1)}) custom-call(s32[8,64]{1,0:T(8,128)} %bitcast.2, f32[8,64]{1,0:T(8,128)} %bitcast.3, bf16[64,1792]{1,0:T(8,128)(2,1)} %tok_hbm.1, bf16[64,1792]{1,0:T(8,128)(2,1)} %gout_hbm.1, ...), custom_call_target="tpu_custom_call" | custom-call | tf_op jit(solution)/shard_map/routed_backward/pallas_call | solution.py:432
  95.6 0.7 copy.12
  96.3 1.6 %convert_element_type.9 = bf16[1,896,1280]{2,1,0:T(8,128)(2,1)} convert(f32[1,896,1280]{2,1,0:T(8,128)S(1)} %get-tuple-element.9) | non-fusion elementwise | flops 1146880 | bytes 6881280 | tf_op jit(solution)/shard_map/convert_element_type | solution.py:443
  97.9 1.6 %convert_element_type.10 = bf16[1,896,1280]{2,1,0:T(8,128)(2,1)} convert(f32[1,896,1280]{2,1,0:T(8,128)S(1)} %get-tuple-element.10) | non-fusion elementwise | flops 1146880 | bytes 6881280 | tf_op jit(solution)/shard_map/convert_element_type | solution.py:443
  99.5 1.6 %convert_element_type.11 = bf16[1,896,1280]{2,1,0:T(8,128)(2,1)} convert(f32[1,896,1280]{2,1,0:T(8,128)S(1)} %get-tuple-element.11) | non-fusion elementwise | flops 1146880 | bytes 6881280 | tf_op jit(solution)/shard_map/convert_element_type | solution.py:443

commit v3 on v2

--- a/solution.py
+++ b/solution.py
@@ -1,5 +1,3 @@
-import functools
-
 import jax
 import jax.numpy as jnp
 from jax import lax
@@ -47,11 +45,11 @@
 def body(
     ids_hbm, comb_hbm, tok_hbm, gout_hbm, wg_ref, wu_ref, wd_ref,
     tg_ref, og_ref, ou_ref, od_ref,
-    ids_ref, comb_ref, tok_ref, gout_ref, wfull, line0, line1, line2, mytab, mytabs, tabs, r_tab, c_tab, a_mat, perm,
-    spk0, spk1, spk2, rx0, rx1, rx2, xg, hg, far_xg, far_hg, gx,
+    ids_ref, comb_ref, tok_ref, gout_ref, wfull, line0, line1, line2, mytab, mytabs, tabs, r_tab, c_tab, w_rows, a_mat, perm,
+    spk0, spk1, spk2, rx0, rx1, rx2, xg, hg, hgt, far_xg, far_hg, gx,
     rr0, rr1, rr2, lr0, lr1, lr2,
     i_loc, w_loc, w_send, w_recv, lt_send, lt_recv, x_send, x_recv, g_send, g_recv,
-    d_send, d_recv, b_send, b_recv, l_send, l_recv, q_send, q_recv, h_send, h_recv,
+    d_send, d_recv, b_send, b_recv, l_send, l_recv, q_send, q_recv, h_send, h_recv, free_sem,
 ):
     lines, spk, rx = (line0, line1, line2), (spk0, spk1, spk2), (rx0, rx1, rx2)
     rr = (rr0, rr1, rr2)
@@ -125,21 +123,27 @@
 
     pl.semaphore_wait(barrier, 37)
 
-    for i in range(1, 4):
-        for p in range(3):
-            to = (d, expert_of(p, (lcoord[p] + i) % 4, jcoord[p]))
-            rows = pl.ds(pl.multiple_of(lcoord[p] * TOK, TOK), TOK)
-            remote(mytabs.at[p], tabs.at[p, lcoord[p]], lt_send.at[p], lt_recv.at[p], to).start()
-            remote(
-                tok_ref.at[:, pl.ds(IN_COLS[p][0], WI[p])],
-                lines[p].at[rows, pl.ds(0, WI[p])],
-                x_send.at[p], x_recv.at[p], to,
-            ).start()
-            remote(
-                gout_ref.at[:, pl.ds(GR_COLS[p][0], WG[p])],
-                lines[p].at[rows, pl.ds(WI[p], WG[p])],
-                g_send.at[p], g_recv.at[p], to,
-            ).start()
+    for kind in range(3):
+        for i in range(1, 4):
+            for p in range(3):
+                to = (d, expert_of(p, (lcoord[p] + i) % 4, jcoord[p]))
+                rows = pl.ds(pl.multiple_of(lcoord[p] * TOK, TOK), TOK)
+                if kind == 0:
+                    remote(
+                        mytabs.at[p], tabs.at[p, lcoord[p]], lt_send.at[p], lt_recv.at[p], to
+                    ).start()
+                elif kind == 1:
+                    remote(
+                        tok_ref.at[:, pl.ds(IN_COLS[p][0], WI[p])],
+                        lines[p].at[rows, pl.ds(0, WI[p])],
+                        x_send.at[p], x_recv.at[p], to,
+                    ).start()
+                else:
+                    remote(
+                        gout_ref.at[:, pl.ds(GR_COLS[p][0], WG[p])],
+                        lines[p].at[rows, pl.ds(WI[p], WG[p])],
+                        g_send.at[p], g_recv.at[p], to,
+                    ).start()
     for w in range(3):
         remote(w_in[w].at[0], wfull.at[w, own_rows], w_send.at[w], w_recv.at[w], partner).start()
 
@@ -157,15 +161,8 @@
     perm[2] = jnp.where(col0 == row0, 1.0, 0.0).astype(BF16)
     perm[3] = jnp.where(col0 == (rxx << 6) + (rz << 4) + (ry << 2) + rk, 1.0, 0.0).astype(BF16)
 
-    def line_wait(p):
+    for p in range(3):
         remote(tabs.at[p, pl.ds(0, 3)], tabs.at[p, pl.ds(0, 3)], lt_send.at[p], lt_recv.at[p], partner).wait_recv()
-        a = lines[p].at[pl.ds(0, 192), pl.ds(0, WI[p])]
-        b = lines[p].at[pl.ds(0, 192), pl.ds(WI[p], WG[p])]
-        remote(a, a, x_send.at[p], x_recv.at[p], partner).wait_recv()
-        remote(b, b, g_send.at[p], g_recv.at[p], partner).wait_recv()
-
-    for p in range(3):
-        line_wait(p)
         table = jnp.concatenate([tabs[p, 0] + tabs[p, 1], tabs[p, 2] + tabs[p, 3]], axis=1)
         jj = lax.broadcasted_iota(jnp.int32, (16, 1), 0)
         if p == 0:
@@ -184,16 +181,17 @@
         r_tab[p] = rank - 1.0
         c_tab[p] = weight
 
-    def dispatch(c):
+    def dispatch(c, start=(0, 0, 0), width=WP):
         crow = c * CH
 
         def send(i, carry2):
             for p in range(3):
                 jj = peer_j(p, i)
                 to = (d, expert_of(p, lcoord[p], jj))
+                cols = pl.ds(start[p], width[p])
                 remote(
-                    spk[p].at[pl.ds(pl.multiple_of(crow + jj * 16, 16), 16)],
-                    rx[p].at[pl.ds(pl.multiple_of(crow + jcoord[p] * 16, 16), 16)],
+                    spk[p].at[pl.ds(pl.multiple_of(crow + jj * 16, 16), 16), cols],
+                    rx[p].at[pl.ds(pl.multiple_of(crow + jcoord[p] * 16, 16), 16), cols],
                     d_send.at[p, c], d_recv.at[p, c], to,
                 ).start()
             return carry2
@@ -201,13 +199,14 @@
         lax.fori_loop(1, 16, send, 0)
         for p in range(3):
             mine = pl.ds(pl.multiple_of(crow + jcoord[p] * 16, 16), 16)
-            rx[p][mine, :] = spk[p][mine, :]
-
-    def give_back(c):
+            cols = slice(start[p], start[p] + width[p])
+            rx[p][mine, cols] = spk[p][mine, cols]
+
+    def give_back(c, which=(0, 1, 2)):
         crow = c * CH
 
         def send(i, carry2):
-            for p in range(3):
+            for p in which:
                 jj = peer_j(p, i)
                 to = (d, expert_of(p, lcoord[p], jj))
                 remote(
@@ -218,12 +217,11 @@
             return carry2
 
         lax.fori_loop(1, 16, send, 0)
-        for p in range(3):
+        for p in which:
             mine = pl.ds(pl.multiple_of(crow + jcoord[p] * 16, 16), 16)
             rr[p][mine, :] = spk[p][mine, 0 : WR[p]]
 
-    def pack(c, carry):
-        crow = pl.multiple_of(c * CH, CH)
+    def pack_rows(c):
         r_i = lax.broadcasted_iota(jnp.int32, (CH, CH), 0)
         s_i = lax.broadcasted_iota(jnp.int32, (CH, CH), 1) >> 6
         want = jnp.where(((r_i >> 2) & 3) == s_i, (r_i & 3) + 4 * c, -100).astype(F32)
@@ -232,20 +230,32 @@
             wt = jnp.broadcast_to(c_tab[p][:, None, :], (16, 16, CH)).reshape(CH, CH)
             hit = rank == want
             one = jnp.where(hit, 1.0, 0.0).astype(BF16)
-            a_mat[p, pl.ds(crow, CH), :] = one
-            w_row = jnp.sum(jnp.where(hit, wt, 0.0), axis=1, keepdims=True)
-            spk[p][pl.ds(crow, CH), 0 : WI[p]] = dot(one, lines[p][:, 0 : WI[p]]).astype(BF16)
-            spk[p][pl.ds(crow, CH), WI[p] : WP[p]] = (
-                dot(one, lines[p][:, WI[p] : WP[p]]) * w_row
+            a_mat[p, c * CH : (c + 1) * CH, :] = one
+            w_rows[p] = jnp.sum(jnp.where(hit, wt, 0.0), axis=1, keepdims=True)
+            spk[p][c * CH : (c + 1) * CH, 0 : WI[p]] = dot(one, lines[p][:, 0 : WI[p]]).astype(BF16)
+
+    def pack_grads(c):
+        for p in range(3):
+            one = a_mat[p, c * CH : (c + 1) * CH, :]
+            spk[p][c * CH : (c + 1) * CH, WI[p] : WP[p]] = (
+                dot(one, lines[p][:, WI[p] : WP[p]]) * w_rows[p]
             ).astype(BF16)
 
-        @pl.when(c < 2)
-        def _():
-            dispatch(c)
-
-        return carry
-
-    lax.fori_loop(0, CHUNKS, pack, 0)
+    for p in range(3):
+        a = lines[p].at[pl.ds(0, 192), pl.ds(0, WI[p])]
+        remote(a, a, x_send.at[p], x_recv.at[p], partner).wait_recv()
+    pack_rows(0)
+    dispatch(0, (0, 0, 0), WI)
+    for p in range(3):
+        b = lines[p].at[pl.ds(0, 192), pl.ds(WI[p], WG[p])]
+        remote(b, b, g_send.at[p], g_recv.at[p], partner).wait_recv()
+    pack_grads(0)
+    dispatch(0, WI, WG)
+    pack_rows(1)
+    pack_grads(1)
+    dispatch(1)
+    pack_rows(2)
+    pack_grads(2)
 
     def clear(n, carry):
         rows = pl.ds(pl.multiple_of(n * 128, 128), 128)
@@ -263,18 +273,17 @@
     far = pl.ds(pl.multiple_of((1 - d) * HALF, 128), HALF)
 
     def far_wait(c):
-        remote(far_xg.at[c], far_xg.at[c], q_send.at[c], q_recv.at[c], partner).wait_recv()
-        remote(far_hg.at[c], far_hg.at[c], h_send.at[c], h_recv.at[c], partner).wait_recv()
-
-    def terms(c, n, carry):
+        remote(far_xg.at[c % 2], far_xg.at[c % 2], q_send.at[c], q_recv.at[c], partner).wait_recv()
+        remote(far_hg.at[c % 2], far_hg.at[c % 2], h_send.at[c], h_recv.at[c], partner).wait_recv()
+
+    def terms(c, n):
         b = c % 2
-        cols = pl.ds(pl.multiple_of(n * 256, 256), 256)
+        cols = slice(n * 256, n * 256 + 256)
         for w in range(3):
             k = w // 2
             w_out[w][0, :, cols] += dot_tn(xg[b, k, :, near], hg[b, w, :, cols]) + dot_tn(
-                far_xg[c, k], far_hg[c, w, :, cols]
+                far_xg[b, k], far_hg[b, w, :, cols]
             )
-        return carry
 
     def compute(c, carry):
         crow = pl.multiple_of(c * CH, CH)
@@ -283,8 +292,9 @@
 
         @pl.when(c >= 2)
         def _():
-            remote(far_xg.at[c - 2], far_xg.at[c - 2], q_send.at[c - 2], q_recv.at[c - 2], partner).wait_send()
-            remote(far_hg.at[c - 2], far_hg.at[c - 2], h_send.at[c - 2], h_recv.at[c - 2], partner).wait_send()
+            remote(far_xg.at[0], far_xg.at[0], q_send.at[0], q_recv.at[0], partner).wait_send()
+            remote(far_hg.at[0], far_hg.at[0], h_send.at[0], h_recv.at[0], partner).wait_send()
+            pl.semaphore_wait(free_sem, 1)
 
         for p in range(3):
             part = rx[p].at[pl.ds(0, 240)]
@@ -305,60 +315,68 @@
                 xg[b, 1, :, g0:g1] = dot(perm[p - 1], rx[p][rows, WI[p] : WP[p]]).astype(BF16)
         for k in range(2):
             remote(
-                xg.at[b, k, :, far], far_xg.at[c, k], q_send.at[c], q_recv.at[c], partner
+                xg.at[b, k, :, far], far_xg.at[b, k], q_send.at[c], q_recv.at[c], partner
             ).start()
 
-        def units(n, carry2):
-            cols = pl.ds(pl.multiple_of(n * 256, 256), 256)
+        def units(n):
+            cols = slice(n * 256, n * 256 + 256)
             gate = dot(xg[b, 0], wfull[0, :, cols])
             up = dot(xg[b, 0], wfull[1, :, cols])
             gh = dot(xg[b, 1], wfull[2, :, cols])
             sig = jax.nn.sigmoid(gate)
             act = gate * sig
             hg[b, 2, :, cols] = (act * up).astype(BF16)
-            hg[b, 0, :, cols] = (gh * up * sig * (1.0 + gate * (1.0 - sig))).astype(BF16)
-            hg[b, 1, :, cols] = (gh * act).astype(BF16)
-            return carry2
-
-        lax.fori_loop(0, TILES, units, 0)
+            grad_gate = (gh * up * sig * (1.0 + gate * (1.0 - sig))).astype(BF16)
+            grad_up = (gh * act).astype(BF16)
+            hg[b, 0, :, cols] = grad_gate
+            hg[b, 1, :, cols] = grad_up
+            hgt[0, cols, :] = grad_gate.T
+            hgt[1, cols, :] = grad_up.T
+
+        for n in range(TILES):
+            units(n)
 
         @pl.when(c == 0)
         def _():
             dispatch(2)
 
         for k in range(3):
-            remote(hg.at[b, k], far_hg.at[c, k], h_send.at[c], h_recv.at[c], partner).start()
-
-        def grads(n, carry2):
-            cols = pl.ds(pl.multiple_of(n * 256, 256), 256)
-            gx[cols, :] = (
-                dot_nt(wfull[0, cols, :], hg[b, 0]) + dot_nt(wfull[1, cols, :], hg[b, 1])
-            ).astype(BF16)
-            return carry2
-
-        lax.fori_loop(0, D // 256, grads, 0)
+            remote(hg.at[b, k], far_hg.at[b, k], h_send.at[c], h_recv.at[c], partner).start()
+
         for p in range(3):
             part = rx[p].at[pl.ds(0, 240)]
             remote(part, part, d_send.at[p, c], d_recv.at[p, c], partner).wait_send()
+            for n in ((0, 1, 2), (3, 4), (5, 6))[p]:
+                tile = slice(n * 256, n * 256 + 256)
+                gx[tile, :] = (
+                    dot(wfull[0, tile, :], hgt[0]) + dot(wfull[1, tile, :], hgt[1])
+                ).astype(BF16)
+            third = slice(*RT_COLS[p])
             back = perm[(2, 0, 3)[p]]
-            spk[p][rows, 0 : WR[p]] = dot_nt(back, gx[RT_COLS[p][0] : RT_COLS[p][1], :]).astype(BF16)
+            spk[p][rows, 0 : WR[p]] = dot_nt(back, gx[third, :]).astype(BF16)
+
+            @pl.when(c == CHUNKS - 1)
+            def _():
+                give_back(CHUNKS - 1, (p,))
 
         @pl.when(c == 0)
         def _():
             far_wait(c)
-            lax.fori_loop(0, TILES, functools.partial(terms, c), 0)
+            for n in range(TILES):
+                terms(0, n)
+            pl.semaphore_signal(free_sem, inc=1, device_id=partner, device_id_type=MESH)
 
         return carry
 
     lax.fori_loop(0, CHUNKS, compute, 0)
-    give_back(CHUNKS - 1)
     far_wait(1)
     far_wait(2)
 
-    def late_terms(i, carry):
-        return terms(1 + i // TILES, i % TILES, carry)
-
-    lax.fori_loop(0, TILES + 2, late_terms, 0)
+    def late_terms(start, stop):
+        for i in range(start, stop):
+            terms(1 + i // TILES, i % TILES)
+
+    late_terms(0, TILES + 1)
 
     for p in range(3):
         for c in range(CHUNKS):
@@ -377,7 +395,7 @@
             pl.ds(pl.multiple_of(lcoord[p] * TOK, TOK), TOK), 0 : WR[p]
         ]
 
-    lax.fori_loop(TILES + 2, 2 * TILES, late_terms, 0)
+    late_terms(TILES + 1, 2 * TILES)
 
     for p in range(3):
         part = lr[p].at[pl.ds(0, 3)]
@@ -398,8 +416,26 @@
         part = lr[p].at[pl.ds(0, 3)]
         remote(part, part, l_send.at[p], l_recv.at[p], partner).wait_send()
     for c in range(1, CHUNKS):
-        remote(far_xg.at[c], far_xg.at[c], q_send.at[c], q_recv.at[c], partner).wait_send()
-        remote(far_hg.at[c], far_hg.at[c], h_send.at[c], h_recv.at[c], partner).wait_send()
+        remote(far_xg.at[c % 2], far_xg.at[c % 2], q_send.at[c], q_recv.at[c], partner).wait_send()
+        remote(far_hg.at[c % 2], far_hg.at[c % 2], h_send.at[c], h_recv.at[c], partner).wait_send()
+
+
+def finish(tg_ref, sg_ref, su_ref, sd_ref, tg_out, g_out, u_out, d_out, g_b, u_b, d_b, t_sem, sem):
+    token = pltpu.make_async_copy(tg_ref, tg_out, t_sem)
+    token.start()
+    groups = ((sg_ref, g_b, g_out), (su_ref, u_b, u_out), (sd_ref, d_b, d_out))
+
+    def tile(n, carry):
+        rows = pl.ds(pl.multiple_of(n * 128, 128), 128)
+        for w, (total, held, out) in enumerate(groups):
+            held[rows, :] = total[0, rows, :].astype(BF16)
+            pltpu.make_async_copy(held.at[rows], out.at[0, rows], sem.at[w]).start()
+        return carry
+
+    lax.fori_loop(0, HALF // 128, tile, 0)
+    for w, (_, held, out) in enumerate(groups):
+        pltpu.make_async_copy(held, out.at[0], sem.at[w]).wait()
+    token.wait()
 
 
 def shards(tokens, grad_out, combine, expert_ids, w_gate, w_up, w_down):
@@ -411,12 +447,12 @@
         v((3, D, FF), BF16),
         *[v((CH, w), BF16) for w in WP],
         v((24, 128), F32), v((3, 24, 128), F32), v((3, 4, 24, 128), F32),
-        v((3, 16, CH), F32), v((3, 16, CH), F32),
+        v((3, 16, CH), F32), v((3, 16, CH), F32), v((3, CH, 1), F32),
         v((3, rows, CH), BF16), v((4, CH, CH), BF16),
         *[v((rows, w), BF16) for w in WP],
         *[v((rows, w), BF16) for w in WP],
-        v((2, 2, CH, D), BF16), v((2, 3, CH, FF), BF16),
-        v((CHUNKS, 2, CH, HALF), BF16), v((CHUNKS, 3, CH, FF), BF16),
+        v((2, 2, CH, D), BF16), v((2, 3, CH, FF), BF16), v((2, FF, CH), BF16),
+        v((2, 2, CH, HALF), BF16), v((2, 3, CH, FF), BF16),
         v((D, CH), BF16),
         *[v((rows, w), BF16) for w in WR],
         *[v((4, TOK, w), BF16) for w in WR],
@@ -427,6 +463,7 @@
         *[dma((3,))] * 9,
         *[dma((3, 3))] * 4,
         *[dma((3,))] * 6,
+        pltpu.SemaphoreType.REGULAR,
     ]
     sums = v((1, HALF, FF), F32)
     token_grad, *grads = pl.pallas_call(
@@ -436,11 +473,21 @@
         out_specs=(vm, vm, vm, vm),
         scratch_shapes=scratch + sems,
         compiler_params=pltpu.CompilerParams(
-            collective_id=0, has_side_effects=True, vmem_limit_bytes=52500000
+            collective_id=0, has_side_effects=True, vmem_limit_bytes=52900000
         ),
         name="routed_backward",
     )(expert_ids.T, combine.T, tokens, grad_out, w_gate, w_up, w_down)
-    return (token_grad, *[g.astype(BF16) for g in grads])
+    hold = [v((HALF, FF), BF16)] * 3
+    return pl.pallas_call(
+        finish,
+        out_shape=[jax.ShapeDtypeStruct((TOK, D), BF16)]
+        + [jax.ShapeDtypeStruct((1, HALF, FF), BF16)] * 3,
+        in_specs=[vm] * 4,
+        out_specs=[hbm] * 4,
+        scratch_shapes=hold + [dma, dma((3,))],
+        compiler_params=pltpu.CompilerParams(vmem_limit_bytes=16 << 20),
+        name="finish",
+    )(token_grad, *grads)
 
 
 def solution(mesh):

time: 102 us -> 92.2 us (0.904)
  other arithmetic: 4.82 us -> 0 us
  Pallas kernels: 94.9 us -> 90.8 us
    pallas_call x1, Pallas kernels: 94.9 us -> 87.9 us  [shards(): pl.pallas_call(body, out_shape=(v((TOK, D), BF16), sums, sums, sums), in_...]
    convert_element_type x3 -> x0, other arithmetic: 4.82 us -> none  [shards(): return (token_grad, *[g.astype(BF16) for g in grads])]
    pallas_call x0 -> x1, Pallas kernels: none -> 2.92 us  [shards(): pl.pallas_call(finish, out_shape=[jax.ShapeDtypeStruct((TOK, D), BF16)] +...]
where the time goes in v3:
time: 92.2 us; the launch traced here: 91.6 us
  Pallas kernels  90.8 us (98%)
    pallas_call x1, Pallas kernels, shards(): pl.pallas_call(body, out_shape=(v((TOK, D), BF16), sums, sums, sums), in_...  87.9 us
    pallas_call x1, Pallas kernels, shards(): pl.pallas_call(finish, out_shape=[jax.ShapeDtypeStruct((TOK, D), BF16)] +...  2.92 us

profile of v3, /device:TPU:1, one launch (start us, length us, event | category | flops | bytes accessed | tf_op | source)
XLA Modules:
  0.0 91.6 jit_solution(12664968305841080786)
XLA Ops:
  0.6 87.9 %routed_backward.1 = (bf16[64,1792]{1,0:T(8,128)(2,1)S(1)}, f32[1,896,1280]{2,1,0:T(8,128)S(1)}, f32[1,896,1280]{2,1,0:T(8,128)S(1)}, f32[1,896,1280]{2,1,0:T(8,128)S(1)}) custom-call(s32[8,64]{1,0:T(8,128)} %bitcast.2, f32[8,64]{1,0:T(8,128)} %bitcast.3, bf16[64,1792]{1,0:T(8,128)(2,1)} %tok_hbm.1, bf16[64,1792]{1,0:T(8,128)(2,1)} %gout_hbm.1, ...), custom_call_target="tpu_custom_call" | custom-call | tf_op jit(solution)/shard_map/routed_backward/pallas_call | solution.py:469
  88.5 2.9 %finish.1 = (bf16[64,1792]{1,0:T(8,128)(2,1)}, bf16[1,896,1280]{2,1,0:T(8,128)(2,1)}, bf16[1,896,1280]{2,1,0:T(8,128)(2,1)}, bf16[1,896,1280]{2,1,0:T(8,128)(2,1)}) custom-call(bf16[64,1792]{1,0:T(8,128)(2,1)S(1)} %get-tuple-element.8.tg_ref, f32[1,896,1280]{2,1,0:T(8,128)S(1)} %get-tuple-element.9.sg_ref, f32[1,896,1280]{2,1,0:T(8,128)S(1)} %get-tuple-element.10.su_ref, ...), custom_call_target="tpu_custom_call" | custom-call | tf_op jit(solution)/shard_map/finish/pallas_call | solution.py:481

commit v4 on v3

--- a/solution.py
+++ b/solution.py
@@ -45,7 +45,7 @@
 def body(
     ids_hbm, comb_hbm, tok_hbm, gout_hbm, wg_ref, wu_ref, wd_ref,
     tg_ref, og_ref, ou_ref, od_ref,
-    ids_ref, comb_ref, tok_ref, gout_ref, wfull, line0, line1, line2, mytab, mytabs, tabs, r_tab, c_tab, w_rows, a_mat, perm,
+    ids_ref, comb_ref, tok_ref, gout_ref, wfull, line0, line1, line2, mytab, mytabs, tabs, r_tab, c_tab, a_mat, perm,
     spk0, spk1, spk2, rx0, rx1, rx2, xg, hg, hgt, far_xg, far_hg, gx,
     rr0, rr1, rr2, lr0, lr1, lr2,
     i_loc, w_loc, w_send, w_recv, lt_send, lt_recv, x_send, x_recv, g_send, g_recv,
@@ -65,6 +65,8 @@
 
     def peer_j(p, i):
         j = jcoord[p]
+        if p == 1:
+            return ((j // 4 + i % 4) % 4) * 4 + (j % 4 + i // 4) % 4
         return ((j // 4 + i // 4) % 4) * 4 + (j % 4 + i % 4) % 4
 
     def remote(src, dst, ss, rsem, device):
@@ -87,9 +89,9 @@
 
     for i in range(1, 16):
         greet(0, i)
-        if i >= 4:
+        if i % 4:
             greet(1, i)
-            if i % 4:
+            if i >= 4:
                 greet(2, i)
     pl.semaphore_signal(barrier, inc=1, device_id=partner, device_id_type=MESH)
 
@@ -227,18 +229,17 @@
         want = jnp.where(((r_i >> 2) & 3) == s_i, (r_i & 3) + 4 * c, -100).astype(F32)
         for p in range(3):
             rank = jnp.broadcast_to(r_tab[p][:, None, :], (16, 16, CH)).reshape(CH, CH)
-            wt = jnp.broadcast_to(c_tab[p][:, None, :], (16, 16, CH)).reshape(CH, CH)
-            hit = rank == want
-            one = jnp.where(hit, 1.0, 0.0).astype(BF16)
+            one = jnp.where(rank == want, 1.0, 0.0).astype(BF16)
             a_mat[p, c * CH : (c + 1) * CH, :] = one
-            w_rows[p] = jnp.sum(jnp.where(hit, wt, 0.0), axis=1, keepdims=True)
             spk[p][c * CH : (c + 1) * CH, 0 : WI[p]] = dot(one, lines[p][:, 0 : WI[p]]).astype(BF16)
 
     def pack_grads(c):
         for p in range(3):
             one = a_mat[p, c * CH : (c + 1) * CH, :]
+            wt = jnp.broadcast_to(c_tab[p][:, None, :], (16, 16, CH)).reshape(CH, CH)
+            w_row = jnp.sum(one.astype(F32) * wt, axis=1, keepdims=True)
             spk[p][c * CH : (c + 1) * CH, WI[p] : WP[p]] = (
-                dot(one, lines[p][:, WI[p] : WP[p]]) * w_rows[p]
+                dot(one, lines[p][:, WI[p] : WP[p]]) * w_row
             ).astype(BF16)
 
     for p in range(3):
@@ -299,10 +300,6 @@
         for p in range(3):
             part = rx[p].at[pl.ds(0, 240)]
             remote(part, part, d_send.at[p, c], d_recv.at[p, c], partner).wait_recv()
-
-        @pl.when(c >= 1)
-        def _():
-            give_back(c - 1)
 
         for p in range(3):
             i0, i1 = IN_COLS[p]
@@ -340,6 +337,10 @@
         def _():
             dispatch(2)
 
+        @pl.when(c == 1)
+        def _():
+            give_back(0)
+
         for k in range(3):
             remote(hg.at[b, k], far_hg.at[b, k], h_send.at[c], h_recv.at[c], partner).start()
 
@@ -358,6 +359,10 @@
             @pl.when(c == CHUNKS - 1)
             def _():
                 give_back(CHUNKS - 1, (p,))
+
+        @pl.when(c == 1)
+        def _():
+            give_back(1)
 
         @pl.when(c == 0)
         def _():
@@ -447,7 +452,7 @@
         v((3, D, FF), BF16),
         *[v((CH, w), BF16) for w in WP],
         v((24, 128), F32), v((3, 24, 128), F32), v((3, 4, 24, 128), F32),
-        v((3, 16, CH), F32), v((3, 16, CH), F32), v((3, CH, 1), F32),
+        v((3, 16, CH), F32), v((3, 16, CH), F32),
         v((3, rows, CH), BF16), v((4, CH, CH), BF16),
         *[v((rows, w), BF16) for w in WP],
         *[v((rows, w), BF16) for w in WP],

time: 92.2 us -> 90.7 us (0.984)
  Pallas kernels: 90.8 us -> 89.4 us
    pallas_call x1, Pallas kernels: 87.9 us -> 86.5 us  [shards(): pl.pallas_call(body, out_shape=(v((TOK, D), BF16), sums, sums, sums), in_...]
where the time goes in v4:
time: 90.7 us; the launch traced here: 90.2 us
  Pallas kernels  89.4 us (99%)
    pallas_call x1, Pallas kernels, shards(): pl.pallas_call(body, out_shape=(v((TOK, D), BF16), sums, sums, sums), in_...  86.5 us
    pallas_call x1, Pallas kernels, shards(): pl.pallas_call(finish, out_shape=[jax.ShapeDtypeStruct((TOK, D), BF16)] +...  2.92 us

profile of v4, /device:TPU:1, one launch (start us, length us, event | category | flops | bytes accessed | tf_op | source)
XLA Modules:
  0.0 90.2 jit_solution(683716709205771633)
XLA Ops:
  0.6 86.5 %routed_backward.1 = (bf16[64,1792]{1,0:T(8,128)(2,1)S(1)}, f32[1,896,1280]{2,1,0:T(8,128)S(1)}, f32[1,896,1280]{2,1,0:T(8,128)S(1)}, f32[1,896,1280]{2,1,0:T(8,128)S(1)}) custom-call(s32[8,64]{1,0:T(8,128)} %bitcast.2, f32[8,64]{1,0:T(8,128)} %bitcast.3, bf16[64,1792]{1,0:T(8,128)(2,1)} %tok_hbm.1, bf16[64,1792]{1,0:T(8,128)(2,1)} %gout_hbm.1, ...), custom_call_target="tpu_custom_call" | custom-call | tf_op jit(solution)/shard_map/routed_backward/pallas_call | solution.py:474
  87.1 2.9 %finish.1 = (bf16[64,1792]{1,0:T(8,128)(2,1)}, bf16[1,896,1280]{2,1,0:T(8,128)(2,1)}, bf16[1,896,1280]{2,1,0:T(8,128)(2,1)}, bf16[1,896,1280]{2,1,0:T(8,128)(2,1)}) custom-call(bf16[64,1792]{1,0:T(8,128)(2,1)S(1)} %get-tuple-element.8.tg_ref, f32[1,896,1280]{2,1,0:T(8,128)S(1)} %get-tuple-element.9.sg_ref, f32[1,896,1280]{2,1,0:T(8,128)S(1)} %get-tuple-element.10.su_ref, ...), custom_call_target="tpu_custom_call" | custom-call | tf_op jit(solution)/shard_map/finish/pallas_call | solution.py:486
